TPU v7x, 256 devices: a whole 4x4x8 slice. The times are simulated.
256 devices in a mesh: scen: 32 (over z, y), tile: 8 (over x, core).
Axes of the slice: x: 4, y: 4, z: 8, core: 2. Of those that a mesh axis runs over, the one named last changes fastest.
Arguments:
- factor_inv: bfloat16 [256, 768, 768], P('scen'), may hold values from -0.21875 to 0.21875
- pattern: int32 [256, 6, 6], P('scen'), may hold values 0 or 1
- border: bfloat16 [256, 768, 1024], P('scen', None, 'tile'), may hold values from -0.59765625 to 0.59765625
- row_scale: float32 [256, 768], P('scen'), may hold values from 0.25 to 4
- link_ids: int32 [256, 8], P('scen'), may hold values from 0 to 63, as said below
- first_diag: float32 [8192], replicated, may hold values from 10 to 100
Outputs:
- schur: float32 [8192, 8192], P('tile', 'scen')
Inputs may be any that keep to these rules, and one draw needn't show every extreme that they name: link_ids[s, j] lies in group j, that is among blocks j * 8 to (j + 1) * 8 - 1. For each aligned block of 8 scenarios and each group, at most 3 of those scenarios link to one run of 2 blocks starting at a multiple of 2, and one such run has exactly 3.
All inputs are finite; a program needn't handle non-finite values. No bound on the sum of `pattern` on one device may be relied on, other than what follows from the above.
Results may differ from a plain program's by a relative error of at most 0.003.
Values may be sent and summed in bfloat16 or wider, within the bound.
No kernel may reach another device: no remote copies, remote signals or barrier semaphores. Data moves between devices by JAX's collectives and lax.ppermute only.
A program may use at most 128 MiB of HBM per device.

v0:
```python
import jax
import jax.numpy as jnp
from jax import lax
from jax.sharding import PartitionSpec as P


def on_device(factor_inv, pattern, border, row_scale, link_ids, first_diag):
    local_scen, scen_rows, _ = factor_inv.shape
    block_count = pattern.shape[1]
    block_size = border.shape[2]
    order_size = first_diag.shape[0]
    tile_count = lax.axis_size("tile")
    owner_count = lax.axis_size("scen")
    tile_id = lax.axis_index("tile")
    owner_id = lax.axis_index("scen")
    group_blocks = order_size // (tile_count * block_size)
    owner_blocks = order_size // (owner_count * block_size)
    owners_group = owner_count // tile_count
    capacity = local_scen // owners_group + local_scen // (2 * owners_group)
    index_blocks = jnp.arange(block_count)
    diagonal_mask = index_blocks[:, None] == index_blocks[None, :]
    below_diag = (index_blocks[:, None] > index_blocks[None, :]).astype(jnp.int32)
    effective = jnp.where(diagonal_mask[None], 1, pattern * below_diag[None])
    shaped = factor_inv.reshape(local_scen, block_count, block_size, block_count, block_size)
    masked = (shaped * effective[:, :, None, :, None].astype(jnp.bfloat16)).reshape(
        local_scen, scen_rows, scen_rows
    )
    solved_own = jnp.einsum(
        "snm,smc->snc", masked, border, preferred_element_type=jnp.float32
    ).astype(jnp.bfloat16)
    scaled = (row_scale[:, :, None] * solved_own.astype(jnp.float32)).astype(jnp.bfloat16)
    row_blocks = jnp.einsum(
        "snr,snc->src",
        scaled,
        lax.all_gather(solved_own, "tile", axis=2, tiled=True),
        preferred_element_type=jnp.float32,
    )
    blocks_out = jnp.transpose(
        row_blocks.reshape(local_scen, block_size, tile_count, block_size), (0, 2, 1, 3)
    )
    destination = link_ids // owner_blocks
    same_owner = destination[:, None, :] == destination[None, :, :]
    scen_index = jnp.arange(local_scen)
    earlier = (scen_index[None, :] < scen_index[:, None])[:, :, None]
    slot_rank = jnp.sum((same_owner & earlier).astype(jnp.int32), axis=1)
    own_links = lax.dynamic_slice_in_dim(link_ids, tile_id, 1, 1)[:, 0]
    row_local = own_links - tile_id * group_blocks
    target = row_local[:, None] * owner_blocks + link_ids % owner_blocks
    bin_count = group_blocks * owner_blocks
    send_blocks = jnp.zeros((owner_count, capacity, block_size, block_size), jnp.float32)
    send_blocks = send_blocks.at[destination, slot_rank].set(blocks_out)
    send_targets = jnp.full((owner_count, capacity), bin_count, jnp.int32)
    send_targets = send_targets.at[destination, slot_rank].set(target)
    received, received_targets = (
        lax.all_to_all(
            send_blocks.astype(jnp.bfloat16), "scen", split_axis=0, concat_axis=0, tiled=True
        ).astype(send_blocks.dtype),
        lax.all_to_all(send_targets, "scen", split_axis=0, concat_axis=0, tiled=True),
    )
    target_bins = jnp.zeros((bin_count + 1, block_size, block_size), jnp.float32)
    target_bins = target_bins.at[received_targets.reshape(-1)].add(
        received.reshape(-1, block_size, block_size)
    )
    tile_rows = group_blocks * block_size
    tile_cols = owner_blocks * block_size
    tile_out = jnp.transpose(
        target_bins[:bin_count].reshape(group_blocks, owner_blocks, block_size, block_size),
        (0, 2, 1, 3),
    ).reshape(tile_rows, tile_cols)
    row_start = tile_id * tile_rows
    col_start = owner_id * tile_cols
    global_rows = row_start + jnp.arange(tile_rows)
    global_cols = col_start + jnp.arange(tile_cols)
    diag_values = lax.dynamic_slice_in_dim(first_diag, row_start, tile_rows)
    on_diagonal = global_rows[:, None] == global_cols[None, :]
    return tile_out + jnp.where(on_diagonal, diag_values[:, None], 0.0)


def solution(mesh):
    in_specs = (
        P("scen", None, None),
        P("scen", None, None),
        P("scen", None, "tile"),
        P("scen", None),
        P("scen", None),
        P(),
    )
    out_specs = P("tile", "scen")
    return jax.shard_map(
        on_device, mesh=mesh, in_specs=in_specs, out_specs=out_specs, check_vma=False
    )
```

profile of v0, /device:TPU:32, one launch (start us, length us, event | category | flops | bytes accessed | tf_op | source)
XLA Modules:
  0.0 266.4 jit_solution(12266501531312780159)
XLA Ops:
  6.5 0.9 select_convert_fusion
  7.4 6.3 %mul.46 = bf16[8,6,128,6,128]{4,3,2,1,0:T(8,128)(2,1)} broadcast(bf16[8,6,6]{2,1,0:T(8,128)(2,1)S(1)} %copy.27), dimensions={0,1,3} | broadcast | bytes 9437760 | tf_op jit(solution)/shard_map/mul | solution.py:25
  13.7 20.4 %mul.47 = bf16[8,768,768]{2,1,0:T(8,128)(2,1)} reshape(bf16[8,6,128,6,128]{4,3,2,1,0:T(8,128)(2,1)} %mul.46) | data formatting | bytes 18874368 | tf_op jit(solution)/shard_map/mul | solution.py:25
  34.0 10.2 %fusion.2 = bf16[8,768,128]{2,1,0:T(8,128)(2,1)} fusion(bf16[8,768,128]{2,1,0:T(8,128)(2,1)S(1)} %copy-done, bf16[8,768,768]{2,1,0:T(8,128)(2,1)} %param.6, bf16[8,768,768]{2,1,0:T(8,128)(2,1)} %mul.47), kind=kOutput, calls=%fused_computation.9 | convolution fusion | flops 1213464576 | bytes 22020096 | tf_op jit(solution)/shard_map/snm,smc->snc/dot_general | solution.py:28
  44.2 0.0 all-gather.2.cloned.1.call-update
  44.3 0.2 multiply_reduce_fusion
  44.4 0.1 fusion.8
  44.5 0.1 convert_reduce_fusion
  44.6 0.1 reshape.125
  44.7 0.1 reshape.127
  44.8 3.5 %scatter_fusion = s32[32,3]{0,1:T(4,128)S(1)} fusion(s32[32,3]{0,1:T(4,128)S(1)} %broadcast_in_dim.29, s32[64]{0:T(128)S(1)} %reshape.125, s32[64]{0:T(128)S(1)} %reshape.127), kind=kCustom, calls=%fused_computation | custom fusion | bytes 1280 | tf_op jit(solution)/shard_map/scatter | solution.py:53
  48.3 0.7 copy.26
  49.0 11.4 %all-to-all-start = ((s32[32,1,3]{2,1,0:T(1,128)}), s32[32,1,3]{2,1,0:T(1,128)S(1)}, u32[]{:S(2)}, u32[]{:S(2)}) async-start(s32[32,1,3]{2,1,0:T(1,128)} %copy.26), calls=%async_computation | async-start | bytes 32768 | tf_op jit(solution)/shard_map/all_to_all | solution.py:58
  60.4 61.3 %all-gather.2.cloned.1.call-done = bf16[8,768,1024]{2,1,0:T(8,128)(2,1)} async-done(((bf16[8,768,128]{2,1,0:T(8,128)(2,1)}), bf16[8,768,1024]{2,1,0:T(8,128)(2,1)}) %all-gather.2.cloned.1.call-update) | async-done | bytes 12582928 | tf_op jit(solution)/shard_map/all_gather | solution.py:35
  121.7 6.3 %convolution_bitcast_fusion = f32[8,16,8,8,128]{4,3,2,1,0:T(8,128)S(1)} fusion(bf16[8,768,1024]{2,1,0:T(8,128)(2,1)} %all-gather.2.cloned.1.call-done, bf16[8,768,128]{2,1,0:T(8,128)(2,1)S(1)} %copy-done.2, f32[8,768]{1,0:T(8,128)S(1)} %copy-done.3), kind=kOutput, calls=%fused_computation.8 | convolution fusion | flops 1612972032 | bytes 18374656 | tf_op jit(solution)/shard_map/snr,snc->src/dot_general | solution.py:32
  128.0 2.6 copy.37
  130.6 3.4 %broadcast_in_dim.31 = f32[32,3,128,128]{3,2,1,0:T(8,128)} broadcast(f32[]{:T(128)} %constant.19.clone.1), dimensions={} | broadcast | bytes 6291460 | tf_op jit(solution)/shard_map/broadcast_in_dim | solution.py:50
  134.0 12.8 %scatter_fusion.1 = f32[32,3,128,128]{3,2,1,0:T(8,128)} fusion(f32[32,3,128,128]{3,2,1,0:T(8,128)} %broadcast_in_dim.31, s32[64]{0:T(128)S(1)} %reshape.125, f32[64,128,128]{2,1,0:T(8,128)} %bitcast.36), kind=kCustom, calls=%fused_computation.1 | custom fusion | bytes 12583424 | tf_op jit(solution)/shard_map/scatter | solution.py:51
  146.8 5.1 %convert_element_type.33 = bf16[32,3,128,128]{3,2,1,0:T(8,128)(2,1)} convert(f32[32,3,128,128]{3,2,1,0:T(8,128)} %scatter_fusion.1) | non-fusion elementwise | flops 1572864 | bytes 9437184 | tf_op jit(solution)/shard_map/convert_element_type | solution.py:56
  151.9 10.0 %all-to-all-start.1 = ((bf16[32,3,128,128]{3,2,1,0:T(8,128)(2,1)}), bf16[32,3,128,128]{3,2,1,0:T(8,128)(2,1)}, u32[]{:S(2)}, u32[]{:S(2)}) async-start(bf16[32,3,128,128]{3,2,1,0:T(8,128)(2,1)} %convert_element_type.33), calls=%async_computation.1 | async-start | bytes 6291456 | tf_op jit(solution)/shard_map/all_to_all | solution.py:55
  162.0 0.5 broadcast.140
  162.5 0.7 reduce.5
  163.2 0.1 reshape.117
  163.3 71.3 %all-to-all-done.1 = bf16[32,3,128,128]{3,2,1,0:T(8,128)(2,1)} async-done(((bf16[32,3,128,128]{3,2,1,0:T(8,128)(2,1)}), bf16[32,3,128,128]{3,2,1,0:T(8,128)(2,1)}, u32[]{:S(2)}, u32[]{:S(2)}) %all-to-all-start.1) | async-done | bytes 3145760 | tf_op jit(solution)/shard_map/all_to_all | solution.py:55
  234.6 5.4 %bitcast_convert_fusion = f32[96,128,128]{2,1,0:T(8,128)} fusion(bf16[32,3,128,128]{3,2,1,0:T(8,128)(2,1)} %all-to-all-done.1), kind=kLoop, calls=%fused_computation.6 | loop fusion | flops 1572864 | bytes 9437184 | tf_op jit(solution)/shard_map/reshape | solution.py:62
  240.0 0.1 broadcast_in_dim.28
  240.1 12.9 %scatter_fusion.2 = f32[17,128,128]{2,1,0:T(8,128)S(1)} fusion(f32[17,128,128]{2,1,0:T(8,128)S(1)} %broadcast_in_dim.28, s32[96]{0:T(128)S(1)} %fusion.14, f32[96,128,128]{2,1,0:T(8,128)} %bitcast_convert_fusion), kind=kCustom, calls=%fused_computation.2 | custom fusion | flops 1572864 | bytes 18874752 | tf_op jit(solution)/shard_map/scatter-add | solution.py:61
  253.0 0.0 dynamic-slice-start
  253.0 1.0 slice.8
  254.1 1.6 copy.30
  255.7 1.3 bitcast_add_fusion
  257.0 2.5 copy.31
  (21 shorter events, 0.1 us)
Async XLA Ops:
  6.5 27.5 %copy-start = (bf16[8,768,128]{2,1,0:T(8,128)(2,1)S(1)}, bf16[8,768,128]{2,1,0:T(8,128)(2,1)}, u32[]{:S(2)}) copy-start(bf16[8,768,128]{2,1,0:T(8,128)(2,1)} %param.8) | copy-start | bytes 4718596
  6.5 115.1 %all-gather.2.cloned.1.call-start = ((), (), s32[]{:S(2)}) async-start(), calls=%async_computation.2 | async-start | bytes 14155776 | tf_op jit(solution)/shard_map/all_gather | solution.py:35
  34.0 10.2 %copy-start.4 = (s32[8,8]{1,0:T(8,128)S(1)}, s32[8,8]{1,0:T(8,128)}, u32[]{:S(2)}) copy-start(s32[8,8]{1,0:T(8,128)} %param.10) | copy-start | bytes 772
  44.8 76.9 %copy-start.2 = (bf16[8,768,128]{2,1,0:T(8,128)(2,1)S(1)}, bf16[8,768,128]{2,1,0:T(8,128)(2,1)}, u32[]{:S(2)}) copy-start(bf16[8,768,128]{2,1,0:T(8,128)(2,1)} %fusion.2) | copy-start | bytes 4718596
  44.8 76.9 %copy-start.3 = (f32[8,768]{1,0:T(8,128)S(1)}, f32[8,768]{1,0:T(8,128)}, u32[]{:S(2)}) copy-start(f32[8,768]{1,0:T(8,128)} %param.9) | copy-start | bytes 73732
  49.0 102.9 %all-to-all-start = ((s32[32,1,3]{2,1,0:T(1,128)}), s32[32,1,3]{2,1,0:T(1,128)S(1)}, u32[]{:S(2)}, u32[]{:S(2)}) async-start(s32[32,1,3]{2,1,0:T(1,128)} %copy.26), calls=%async_computation | async-start | bytes 32768 | tf_op jit(solution)/shard_map/all_to_all | solution.py:58
  151.9 82.7 %all-to-all-start.1 = ((bf16[32,3,128,128]{3,2,1,0:T(8,128)(2,1)}), bf16[32,3,128,128]{3,2,1,0:T(8,128)(2,1)}, u32[]{:S(2)}, u32[]{:S(2)}) async-start(bf16[32,3,128,128]{3,2,1,0:T(8,128)(2,1)} %convert_element_type.33), calls=%async_computation.1 | async-start | bytes 6291456 | tf_op jit(solution)/shard_map/all_to_all | solution.py:55
  240.1 19.4 %copy-start.1 = (bf16[8,768,128]{2,1,0:T(8,128)(2,1)S(1)}, bf16[8,768,128]{2,1,0:T(8,128)(2,1)}, u32[]{:S(2)}) copy-start(bf16[8,768,128]{2,1,0:T(8,128)(2,1)} %param.8) | copy-start | bytes 4718596
  253.0 2.7 %dynamic-slice-start = ((f32[8192]{0:T(1024)}, s32[]{:T(128)}), f32[1024]{0:T(1024)S(1)}, s32[]{:S(2)}) async-start(f32[8192]{0:T(1024)} %param.11, s32[]{:T(128)} %select_n.58), calls=%async_computation.3 | async-start | bytes 8704 | tf_op jit(solution)/shard_map/dynamic_slice | solution.py:74
Sparse Core Ops, SparseCore 0:
  44.4 77.2 all-gather.1
where the time goes:
time: 269 us; the launch traced here: 266 us
  waiting for transfers between devices  133 us (49%)
  local copies, waits for them, and re-layouts  55.7 us (21%)
  other arithmetic  26.6 us (10%)
  starting transfers between devices  21.4 us (8%)
  matrix products  16.5 us (6%)
  between operations  13.6 us (5%)
    all_to_all x1, waiting for transfers between devices, on_device(): lax.all_to_all(send_blocks.astype(jnp.bfloat16), 'scen', split_axis=0, co...  71.3 us
    all_gather x1, waiting for transfers between devices, on_device(): lax.all_gather(solved_own, 'tile', axis=2, tiled=True)  61.3 us
    mul x2, local copies, waits for them, and re-layouts, on_device(): shaped * effective[:, :, None, :, None].astype(jnp.bfloat16)  26.6 us
    scatter-add x1, other arithmetic, on_device(): target_bins.at[received_targets.reshape(-1)]  12.9 us
    scatter x1, local copies, waits for them, and re-layouts, on_device(): send_blocks = send_blocks.at[destination, slot_rank].set(blocks_out)  12.8 us
    all_to_all x1, starting transfers between devices, on_device(): lax.all_to_all(send_targets, 'scen', split_axis=0, concat_axis=0, tiled=T...  11.4 us
    dot_general x1, matrix products, on_device(): jnp.einsum('snm,smc->snc', masked, border, preferred_element_type=jnp.flo...  10.2 us
    all_to_all x1, starting transfers between devices, on_device(): lax.all_to_all(send_blocks.astype(jnp.bfloat16), 'scen', split_axis=0, co...  10 us
  transfers between devices with their start and end apart: 3, of which 2 were waited for; matrix products, arithmetic and copies ran while one was open for 14% of the time, Pallas kernels for 0%

commit v1 on v0

v1 whole, which is shorter than its diff:
```python
import jax
import jax.numpy as jnp
from jax import lax
from jax.experimental import pallas as pl
from jax.experimental.pallas import tpu as pltpu
from jax.sharding import Mesh, PartitionSpec as P

BF = jnp.bfloat16
F32 = jnp.float32


def pair_kernel(tile_ref, pattern_ref, factor_ref, border_ref, scale_ref, out_ref, solved_ref, scaled_ref):
    groups, rows, bs = border_ref.shape
    nblk = rows // bs
    tile = tile_ref[0]
    for a in range(nblk):
        lo, hi = a * bs, (a + 1) * bs
        parts = []
        for b in range(a + 1):
            block = factor_ref[0, lo:hi, b * bs:(b + 1) * bs]
            if b < a:
                keep = pattern_ref[tile, a * nblk + b] != 0
                block = jnp.where(keep, block, jnp.zeros_like(block))
            parts.append(block)
        masked = jnp.concatenate(parts, axis=1)
        scale = scale_ref[lo:hi, :]
        for g in range(0, groups, 2):
            rhs = jnp.concatenate([border_ref[g, :hi, :], border_ref[g + 1, :hi, :]], axis=1)
            solved = jnp.dot(masked, rhs, preferred_element_type=F32).astype(BF)
            solved_ref[lo:hi, g * bs:(g + 2) * bs] = solved
            scaled_ref[lo:hi, g * bs:(g + 2) * bs] = (scale * solved.astype(F32)).astype(BF)
    for i in range(0, groups, 2):
        lhs = scaled_ref[:, i * bs:(i + 2) * bs]
        for j in range(0, groups, 2):
            rhs = solved_ref[:, j * bs:(j + 2) * bs]
            pair = lax.dot_general(
                lhs, rhs, (((0,), (0,)), ((), ())), preferred_element_type=F32
            ).astype(BF)
            for di in range(2):
                for dj in range(2):
                    out_ref[(j + dj) * groups + i + di] = pair[
                        di * bs:(di + 1) * bs, dj * bs:(dj + 1) * bs
                    ]


def bin_kernel(target_ref, blocks_ref, out_ref, acc_ref):
    acc_ref[...] = jnp.zeros_like(acc_ref)

    def add(k, carry):
        t = target_ref[k]
        acc_ref[t] += blocks_ref[k].astype(F32)
        return carry

    lax.fori_loop(0, blocks_ref.shape[0], add, 0)
    out_ref[...] = acc_ref[...].astype(BF)


def final_kernel(where_ref, parts_ref, diag_ref, out_ref):
    sources, _, bs, _ = parts_ref.shape
    row_blocks = out_ref.shape[0] // bs
    col_blocks = out_ref.shape[1] // bs
    first_row = where_ref[0]
    first_col = where_ref[1]
    eye = lax.broadcasted_iota(jnp.int32, (bs, bs), 0) == lax.broadcasted_iota(jnp.int32, (bs, bs), 1)
    for r in range(row_blocks):
        for c in range(col_blocks):
            total = parts_ref[0, r * col_blocks + c].astype(F32)
            for s in range(1, sources):
                total = total + parts_ref[s, r * col_blocks + c].astype(F32)
            diag = diag_ref[pl.ds(first_row + r, 1), :]
            on = jnp.logical_and(eye, first_row + r == first_col + c)
            total = total + jnp.where(on, jnp.broadcast_to(diag, (bs, bs)), 0.0)
            out_ref[r * bs:(r + 1) * bs, c * bs:(c + 1) * bs] = total


VMEM = pl.BlockSpec(memory_space=pltpu.VMEM)
SMEM = pl.BlockSpec(memory_space=pltpu.SMEM)


def on_device(factor_inv, pattern, border, row_scale, link_ids, first_diag):
    local_scen, rows, _ = factor_inv.shape
    nblk = pattern.shape[1]
    bs = border.shape[2]
    groups = link_ids.shape[1]
    tile = lax.axis_index(("x", "core"))
    z = lax.axis_index("z")
    y = lax.axis_index("y")
    y_count = lax.axis_size("y")
    order_blocks = first_diag.shape[0] // bs
    group_blocks = order_blocks // groups
    own_cols = group_blocks // y_count

    links = lax.all_gather(link_ids, "z", axis=0, tiled=True)
    borders = lax.all_to_all(border, ("x", "core"), 0, 0, tiled=True)

    scale = lax.dynamic_slice_in_dim(row_scale, tile, 1, 0).reshape(rows, 1)
    pairs = pl.pallas_call(
        pair_kernel,
        out_shape=jax.ShapeDtypeStruct((groups * groups, bs, bs), BF),
        grid_spec=pltpu.PrefetchScalarGridSpec(
            num_scalar_prefetch=2,
            grid=(1,),
            in_specs=[
                pl.BlockSpec((1, rows, rows), lambda i, t, p: (t[0], 0, 0)),
                pl.BlockSpec((groups, rows, bs), lambda i, t, p: (0, 0, 0)),
                pl.BlockSpec((rows, 1), lambda i, t, p: (0, 0)),
            ],
            out_specs=pl.BlockSpec((groups * groups, bs, bs), lambda i, t, p: (0, 0, 0)),
            scratch_shapes=[pltpu.VMEM((rows, groups * bs), BF), pltpu.VMEM((rows, groups * bs), BF)],
        ),
        compiler_params=pltpu.CompilerParams(vmem_limit_bytes=40 << 20),
        name="pair",
    )(tile.reshape(1), pattern.reshape(local_scen, nblk * nblk), factor_inv, borders, scale)

    received = lax.all_to_all(pairs, ("z", "x", "core"), 0, 0, tiled=True)

    row_bin = lax.dynamic_slice_in_dim(links, tile, 1, 1)[:, 0] - tile * group_blocks
    col_bin = lax.dynamic_slice_in_dim(links, z, 1, 1)[:, 0] - z * group_blocks
    target = (col_bin // own_cols) * (group_blocks * own_cols) + row_bin * own_cols + col_bin % own_cols
    bins = pl.pallas_call(
        bin_kernel,
        out_shape=jax.ShapeDtypeStruct((group_blocks * group_blocks, bs, bs), BF),
        in_specs=[SMEM, VMEM],
        out_specs=VMEM,
        scratch_shapes=[pltpu.VMEM((group_blocks * group_blocks, bs, bs), F32)],
        compiler_params=pltpu.CompilerParams(vmem_limit_bytes=40 << 20),
        name="bins",
    )(target, received)

    parts = lax.all_to_all(
        bins.reshape(y_count, group_blocks * own_cols, bs, bs), "y", 0, 0, tiled=True
    )
    place = jnp.stack([tile * group_blocks, z * group_blocks + y * own_cols])
    return pl.pallas_call(
        final_kernel,
        out_shape=jax.ShapeDtypeStruct((group_blocks * bs, own_cols * bs), F32),
        in_specs=[SMEM, VMEM, VMEM],
        out_specs=VMEM,
        compiler_params=pltpu.CompilerParams(vmem_limit_bytes=40 << 20),
        name="final",
    )(place, parts, first_diag.reshape(order_blocks, bs))


def solution(mesh):
    chips = Mesh(mesh.devices.reshape(8, 4, 4, 2), ("z", "y", "x", "core"))
    scen, tile = ("z", "y"), ("x", "core")
    in_specs = (
        P(scen, None, None),
        P(scen, None, None),
        P(scen, None, tile),
        P(scen, None),
        P(scen, None),
        P(),
    )
    return jax.shard_map(
        on_device, mesh=chips, in_specs=in_specs, out_specs=P(tile, scen), check_vma=False
    )
```

time: 269 us -> 142 us (0.53)
  waiting for transfers between devices: 133 us -> 42.2 us
  blocking collectives: 0 us -> 66.8 us
  local copies, waits for them, and re-layouts: 55.7 us -> 5.31 us
  other arithmetic: 26.6 us -> 0.28 us
  matrix products: 16.5 us -> 0 us
  between operations: 13.6 us -> 0.08 us
  Pallas kernels: 0 us -> 8.07 us
    all_gather x0 -> x1, blocking collectives: none -> 66.8 us  [on_device(): links = lax.all_gather(link_ids, 'z', axis=0, tiled=True)]
    all_gather x1 -> x0, waiting for transfers between devices: 61.3 us -> none  [on_device(): lax.all_gather(solved_own, 'tile', axis=2, tiled=True)]
    all_to_all x2 -> x3, waiting for transfers between devices: 71.3 us -> 42.2 us  [the longest x1 21.3 us: on_device(): borders = lax.all_to_all(border, ('x', 'core'), 0, 0, tiled=True)]
    mul x2 -> x0, local copies, waits for them, and re-layouts: 26.6 us -> none  [on_device(): shaped * effective[:, :, None, :, None].astype(jnp.bfloat16)]
    dot_general x2 -> x0, matrix products: 16.5 us -> none  [the longest x1 10.2 us: on_device(): jnp.einsum('snm,smc->snc', masked, border, preferred_element_type=jnp.flo...]
    scatter x2 -> x0, local copies, waits for them, and re-layouts: 16.3 us -> none  [the longest x1 12.8 us: on_device(): send_blocks = send_blocks.at[destination, slot_rank].set(blocks_out)]
    scatter-add x1 -> x0, other arithmetic: 12.9 us -> none  [on_device(): target_bins.at[received_targets.reshape(-1)]]
    pallas_call x0 -> x3, Pallas kernels: none -> 8.07 us  [the longest x1 4.58 us: on_device(): pl.pallas_call(pair_kernel, out_shape=jax.ShapeDtypeStruct((groups * grou...]
  transfers between devices with their start and end apart: 3 -> 3, of which waited for: 2 -> 2; matrix products, arithmetic and copies ran while one was open for 14% -> 0% of each run, Pallas kernels for 0% -> 0%
where the time goes in v1:
time: 142 us
  blocking collectives  66.8 us (47%)
  waiting for transfers between devices  42.2 us (30%)
  starting transfers between devices  18.9 us (13%)
  Pallas kernels  8.07 us (6%)
  local copies, waits for them, and re-layouts  5.31 us (4%)
    all_gather x1, blocking collectives, on_device(): links = lax.all_gather(link_ids, 'z', axis=0, tiled=True)  66.8 us
    all_to_all x1, waiting for transfers between devices, on_device(): borders = lax.all_to_all(border, ('x', 'core'), 0, 0, tiled=True)  21.3 us
    all_to_all x1, waiting for transfers between devices, on_device(): lax.all_to_all(bins.reshape(y_count, group_blocks * own_cols, bs, bs), 'y...  20.9 us
    all_to_all x1, starting transfers between devices, on_device(): received = lax.all_to_all(pairs, ('z', 'x', 'core'), 0, 0, tiled=True)  9.87 us
    unnamed x13, local copies, waits for them, and re-layouts  5.05 us
    all_to_all x1, starting transfers between devices, on_device(): lax.all_to_all(bins.reshape(y_count, group_blocks * own_cols, bs, bs), 'y...  4.6 us
    pallas_call x1, Pallas kernels, on_device(): pl.pallas_call(pair_kernel, out_shape=jax.ShapeDtypeStruct((groups * grou...  4.58 us
    all_to_all x1, starting transfers between devices, on_device(): borders = lax.all_to_all(border, ('x', 'core'), 0, 0, tiled=True)  4.43 us
  transfers between devices with their start and end apart: 3, of which 2 were waited for; matrix products, arithmetic and copies ran while one was open for 0% of the time, Pallas kernels for 0%

profile of v1, /device:TPU:32, one launch (start us, length us, event | category | flops | bytes accessed | tf_op | source)
XLA Modules:
  0.0 141.6 jit_solution(9542323914290036882)
XLA Ops:
  0.0 0.0 copy-start
  0.0 0.0 copy-start.4
  0.0 4.4 %all-to-all-start = ((bf16[8,768,128]{2,1,0:T(8,128)(2,1)}), bf16[8,768,128]{2,1,0:T(8,128)(2,1)S(1)}, u32[]{:S(2)}, u32[]{:S(2)}) async-start(bf16[8,768,128]{2,1,0:T(8,128)(2,1)} %param.8), calls=%async_computation | async-start | bytes 3145728 | tf_op jit(solution)/shard_map/all_to_all | solution.py:94
  4.4 0.0 copy-done.4
  4.5 0.1 reshape.22.pattern_ref
  4.5 0.0 copy-done
  4.5 0.2 copy.9.scale_ref
  4.7 21.3 %all-to-all-done.border_ref = bf16[8,768,128]{2,1,0:T(8,128)(2,1)S(1)} async-done(((bf16[8,768,128]{2,1,0:T(8,128)(2,1)}), bf16[8,768,128]{2,1,0:T(8,128)(2,1)S(1)}, u32[]{:S(2)}, u32[]{:S(2)}) %all-to-all-start) | async-done | bytes 1572896 | tf_op jit(solution)/shard_map/all_to_all | solution.py:94
  26.0 0.0 copy-start.1
  26.0 3.7 %copy-done.1 = bf16[8,768,768]{2,1,0:T(8,128)(2,1)S(1)} copy-done((bf16[8,768,768]{2,1,0:T(8,128)(2,1)S(1)}, bf16[8,768,768]{2,1,0:T(8,128)(2,1)}, u32[]{:S(2)}) %copy-start.1) | copy-done | bytes 9437208
  29.7 4.6 %pair.1 = bf16[64,128,128]{2,1,0:T(8,128)(2,1)} custom-call(s32[1]{0:T(128)} %bitcast.2.tile_ref, s32[8,36]{1,0:T(8,128)S(1)} %reshape.22.pattern_ref, bf16[8,768,768]{2,1,0:T(8,128)(2,1)S(1)} %copy-done.1, bf16[8,768,128]{2,1,0:T(8,128)(2,1)S(1)} %all-to-all-done.border_ref, f32[768,1]{1,0:T(8,128)S(1)} %copy.9.scale_ref), custom_call_target="tpu_custom_call" | custom-call | tf_op jit(solution)/shard_map/pair/pallas_call | solution.py:97
  34.3 0.0 copy-start.5
  34.3 9.9 %all-to-all-start.1 = ((bf16[64,128,128]{2,1,0:T(8,128)(2,1)}), bf16[64,128,128]{2,1,0:T(8,128)(2,1)S(1)}, u32[]{:S(2)}, u32[]{:S(2)}) async-start(bf16[64,128,128]{2,1,0:T(8,128)(2,1)} %pair.1), calls=%async_computation.1 | async-start | bytes 4194304 | tf_op jit(solution)/shard_map/all_to_all | solution.py:115
  44.2 0.0 copy-done.5
  44.2 66.8 %all_gather.3 = s32[64,8]{1,0:T(8,128)S(1)} all-gather(s32[8,8]{1,0:T(8,128)S(1)} %copy-done.5), channel_id=1, replica_groups=mesh['z'=8,'y'=4,'x'=4,'core'=2] {'z'}, dimensions={0}, use_global_device_ids=true | all-gather | bytes 2304 | tf_op jit(solution)/shard_map/all_gather | solution.py:93
  111.0 0.2 subtract_reduce_fusion
  111.2 0.0 all-to-all-done.1.blocks_ref
  111.2 1.7 %bins.1 = bf16[64,128,128]{2,1,0:T(8,128)(2,1)S(1)} custom-call(s32[64]{0:T(128)S(1)} %fusion.target_ref, bf16[64,128,128]{2,1,0:T(8,128)(2,1)S(1)} %all-to-all-done.1.blocks_ref), custom_call_target="tpu_custom_call" | custom-call | tf_op jit(solution)/shard_map/bins/pallas_call | solution.py:120
  112.9 0.0 copy-start.2
  112.9 1.3 copy-done.2
  114.2 0.0 copy-start.3
  114.2 4.6 %all-to-all-start.2 = ((bf16[4,16,128,128]{3,2,1,0:T(8,128)(2,1)}), bf16[4,16,128,128]{3,2,1,0:T(8,128)(2,1)S(1)}, u32[]{:S(2)}, u32[]{:S(2)}) async-start(bf16[4,16,128,128]{3,2,1,0:T(8,128)(2,1)} %bitcast.7), calls=%async_computation.2 | async-start | bytes 4194304 | tf_op jit(solution)/shard_map/all_to_all | solution.py:130
  118.8 0.1 pad_add_fusion.where_ref
  118.9 20.9 %all-to-all-done.2.parts_ref = bf16[4,16,128,128]{3,2,1,0:T(8,128)(2,1)S(1)} async-done(((bf16[4,16,128,128]{3,2,1,0:T(8,128)(2,1)}), bf16[4,16,128,128]{3,2,1,0:T(8,128)(2,1)S(1)}, u32[]{:S(2)}, u32[]{:S(2)}) %all-to-all-start.2) | async-done | bytes 2097184 | tf_op jit(solution)/shard_map/all_to_all | solution.py:130
  139.8 0.0 copy-done.3
  139.8 1.8 %final.1 = f32[1024,256]{1,0:T(8,128)} custom-call(s32[2]{0:T(128)S(1)} %pad_add_fusion.where_ref, bf16[4,16,128,128]{3,2,1,0:T(8,128)(2,1)S(1)} %all-to-all-done.2.parts_ref, f32[64,128]{1,0:T(8,128)S(1)} %bitcast.8), custom_call_target="tpu_custom_call" | custom-call | tf_op jit(solution)/shard_map/final/pallas_call | solution.py:134
  (3 shorter events, 0.0 us)
Async XLA Ops:
  0.0 4.5 %copy-start = (f32[8,768]{1,0:T(8,128)S(1)}, f32[8,768]{1,0:T(8,128)}, u32[]{:S(2)}) copy-start(f32[8,768]{1,0:T(8,128)} %param.9) | copy-start | bytes 73732
  0.0 4.4 %copy-start.4 = (s32[8,6,6]{2,0,1:T(8,128)S(1)}, s32[8,6,6]{2,0,1:T(8,128)}, u32[]{:S(2)}) copy-start(s32[8,6,6]{2,0,1:T(8,128)} %param.7) | copy-start | bytes 3460
  0.0 26.0 %all-to-all-start = ((bf16[8,768,128]{2,1,0:T(8,128)(2,1)}), bf16[8,768,128]{2,1,0:T(8,128)(2,1)S(1)}, u32[]{:S(2)}, u32[]{:S(2)}) async-start(bf16[8,768,128]{2,1,0:T(8,128)(2,1)} %param.8), calls=%async_computation | async-start | bytes 3145728 | tf_op jit(solution)/shard_map/all_to_all | solution.py:94
  26.0 3.7 %copy-start.1 = (bf16[8,768,768]{2,1,0:T(8,128)(2,1)S(1)}, bf16[8,768,768]{2,1,0:T(8,128)(2,1)}, u32[]{:S(2)}) copy-start(bf16[8,768,768]{2,1,0:T(8,128)(2,1)} %factor_ref.1) | copy-start | bytes 28311556
  34.3 9.9 %copy-start.5 = (s32[8,8]{1,0:T(8,128)S(1)}, s32[8,8]{1,0:T(8,128)}, u32[]{:S(2)}) copy-start(s32[8,8]{1,0:T(8,128)} %param.10) | copy-start | bytes 772
  34.3 76.9 %all-to-all-start.1 = ((bf16[64,128,128]{2,1,0:T(8,128)(2,1)}), bf16[64,128,128]{2,1,0:T(8,128)(2,1)S(1)}, u32[]{:S(2)}, u32[]{:S(2)}) async-start(bf16[64,128,128]{2,1,0:T(8,128)(2,1)} %pair.1), calls=%async_computation.1 | async-start | bytes 4194304 | tf_op jit(solution)/shard_map/all_to_all | solution.py:115
  112.9 1.3 copy-start.2
  114.2 25.6 %copy-start.3 = (f32[8192]{0:T(1024)S(1)}, f32[8192]{0:T(1024)}, u32[]{:S(2)}) copy-start(f32[8192]{0:T(1024)} %param.11) | copy-start | bytes 98308
  114.2 25.6 %all-to-all-start.2 = ((bf16[4,16,128,128]{3,2,1,0:T(8,128)(2,1)}), bf16[4,16,128,128]{3,2,1,0:T(8,128)(2,1)S(1)}, u32[]{:S(2)}, u32[]{:S(2)}) async-start(bf16[4,16,128,128]{3,2,1,0:T(8,128)(2,1)} %bitcast.7), calls=%async_computation.2 | async-start | bytes 4194304 | tf_op jit(solution)/shard_map/all_to_all | solution.py:130

commit v2 on v1

v2 whole, which is shorter than its diff:
```python
import jax
import jax.numpy as jnp
from jax import lax
from jax.experimental import pallas as pl
from jax.experimental.pallas import tpu as pltpu
from jax.sharding import Mesh, PartitionSpec as P

BF = jnp.bfloat16
F32 = jnp.float32
TAG = 8

VMEM = pl.BlockSpec(memory_space=pltpu.VMEM)
SMEM = pl.BlockSpec(memory_space=pltpu.SMEM)
HBM = pl.BlockSpec(memory_space=pltpu.HBM)
PARAMS = pltpu.CompilerParams(vmem_limit_bytes=32 << 20)
WIDE = pltpu.CompilerParams(vmem_limit_bytes=60 << 20)


def mask_kernel(tile_ref, pattern_ref, factor_hbm, out_ref, buf_ref, sems):
    rows = buf_ref.shape[0]
    nblk = sems.shape[0]
    bs = rows // nblk
    tile = tile_ref[0]
    copies = [
        pltpu.make_async_copy(
            factor_hbm.at[tile, pl.ds(a * bs, bs), :], buf_ref.at[pl.ds(a * bs, bs), :], sems.at[a]
        )
        for a in range(nblk)
    ]
    for copy in copies:
        copy.start()
    for a in range(nblk):
        copies[a].wait()
        lo, hi = a * bs, (a + 1) * bs
        for b in range(nblk):
            block = buf_ref[lo:hi, b * bs:(b + 1) * bs]
            if b < a:
                keep = pattern_ref[tile, a * nblk + b] != 0
                block = jnp.where(keep, block, jnp.zeros_like(block))
            if b > a:
                block = jnp.zeros_like(block)
            out_ref[lo:hi, b * bs:(b + 1) * bs] = block


def pair_kernel(shift_ref, link_ref, masked_ref, border_ref, scale_ref, out_ref, solved_ref, scaled_ref):
    groups, rows, bs = border_ref.shape
    tile, own_cols, bins_y, group_blocks = (shift_ref[k] for k in range(4))
    for g in range(0, groups, 2):
        rhs = jnp.concatenate([border_ref[g], border_ref[g + 1]], axis=1)
        for a in range(0, rows, 2 * bs):
            lo, hi = a, a + 2 * bs
            solved = jnp.dot(
                masked_ref[lo:hi, :hi], rhs[:hi], preferred_element_type=F32
            ).astype(BF)
            solved_ref[lo:hi, g * bs:(g + 2) * bs] = solved
            scaled_ref[lo:hi, g * bs:(g + 2) * bs] = (
                scale_ref[lo:hi, :] * solved.astype(F32)
            ).astype(BF)
    for i in range(groups):
        row_bin = link_ref[tile, i] - i * group_blocks
        for j in range(groups):
            col_bin = link_ref[tile, j] - j * group_blocks
            owner = lax.div(col_bin, own_cols)
            target = owner * bins_y + row_bin * own_cols + (col_bin - owner * own_cols)
            out_ref[i * groups + j, bs:, :] = jnp.full((TAG, bs), target.astype(F32)).astype(BF)
    for i in range(0, groups, 2):
        lhs = scaled_ref[:, i * bs:(i + 2) * bs]
        for j in range(0, groups, 2):
            rhs = solved_ref[:, j * bs:(j + 2) * bs]
            pair = lax.dot_general(
                lhs, rhs, (((0,), (0,)), ((), ())), preferred_element_type=F32
            ).astype(BF)
            for di in range(2):
                for dj in range(2):
                    out_ref[(i + di) * groups + j + dj, :bs, :] = pair[
                        di * bs:(di + 1) * bs, dj * bs:(dj + 1) * bs
                    ]


def bin_kernel(blocks_hbm, out_hbm, acc_ref, tag_ref, in_ref, buf_ref, meta_ref, target_ref, in_sems, out_sems):
    chunks = in_sems.shape[0] - 2
    count, bs, _ = in_ref.shape
    size = count // chunks
    tags = pltpu.make_async_copy(blocks_hbm.at[:, pl.ds(bs, TAG), :], tag_ref, in_sems.at[chunks])
    tags.start()
    loads = [
        pltpu.make_async_copy(
            blocks_hbm.at[pl.ds(c * size, size), pl.ds(0, bs), :],
            in_ref.at[pl.ds(c * size, size)],
            in_sems.at[c],
        )
        for c in range(chunks)
    ]
    for load in loads:
        load.start()
    tags.wait()
    lane = lax.broadcasted_iota(jnp.int32, (TAG, bs), 1)
    meta = jnp.zeros((TAG, bs), F32)
    for k in range(count):
        meta = jnp.where(lane == k, tag_ref[k].astype(F32), meta)
    meta_ref[...] = meta.astype(jnp.int32)
    targets = pltpu.make_async_copy(meta_ref, target_ref, in_sems.at[chunks + 1])
    targets.start()
    acc_ref[...] = jnp.zeros_like(acc_ref)
    targets.wait()
    for c in range(chunks):
        loads[c].wait()
        for k in range(c * size, (c + 1) * size):
            acc_ref[target_ref[0, k]] += in_ref[k].astype(F32)
    parts, per = buf_ref.shape[:2]
    stores = []
    for p in range(parts):
        buf_ref[p] = acc_ref[p * per:(p + 1) * per].astype(BF)
        store = pltpu.make_async_copy(buf_ref.at[p], out_hbm.at[p], out_sems.at[p])
        store.start()
        stores.append(store)
    for store in stores:
        store.wait()


def final_kernel(where_ref, diag_ref, *rest):
    parts_refs, out_ref = rest[:-1], rest[-1]
    sources, _, _, bs = parts_refs[0].shape
    row_blocks = out_ref.shape[0] // bs
    col_blocks = out_ref.shape[1] // bs
    first_row = where_ref[0]
    first_col = where_ref[1]
    for r in range(row_blocks):
        diag = diag_ref[pl.ds(first_row + r, 1), :]
        for c in range(col_blocks):
            here = first_row + r == first_col + c
            start = 0
            for parts_ref in parts_refs:
                size = parts_ref.shape[2]
                total = parts_ref[0, r * col_blocks + c].astype(F32)
                for s in range(1, sources):
                    total = total + parts_ref[s, r * col_blocks + c].astype(F32)
                eye = (
                    lax.broadcasted_iota(jnp.int32, (size, bs), 0) + start
                    == lax.broadcasted_iota(jnp.int32, (size, bs), 1)
                )
                on = jnp.logical_and(eye, here)
                total = total + jnp.where(on, jnp.broadcast_to(diag, (size, bs)), 0.0)
                out_ref[r * bs + start:r * bs + start + size, c * bs:(c + 1) * bs] = total
                start += size


def on_device(factor_inv, pattern, border, row_scale, link_ids, first_diag):
    local_scen, rows, _ = factor_inv.shape
    nblk = pattern.shape[1]
    bs = border.shape[2]
    groups = link_ids.shape[1]
    tile = lax.axis_index(("x", "core"))
    z = lax.axis_index("z")
    y = lax.axis_index("y")
    y_count = lax.axis_size("y")
    order_blocks = first_diag.shape[0] // bs
    group_blocks = order_blocks // groups
    own_cols = group_blocks // y_count
    bins_y = group_blocks * own_cols

    borders = lax.all_to_all(border, ("x", "core"), 0, 0, tiled=True)

    masked = pl.pallas_call(
        mask_kernel,
        out_shape=jax.ShapeDtypeStruct((rows, rows), BF),
        in_specs=[SMEM, SMEM, HBM],
        out_specs=VMEM,
        scratch_shapes=[pltpu.VMEM((rows, rows), BF), pltpu.SemaphoreType.DMA((nblk,))],
        compiler_params=PARAMS,
        name="mask",
    )(tile.reshape(1), pattern.reshape(local_scen, nblk * nblk), factor_inv)
    scale = lax.dynamic_slice_in_dim(row_scale, tile, 1, 0).reshape(rows, 1)
    shift = jnp.stack([tile, jnp.int32(own_cols), jnp.int32(bins_y), jnp.int32(group_blocks)])
    pairs = pl.pallas_call(
        pair_kernel,
        out_shape=jax.ShapeDtypeStruct((groups * groups, bs + TAG, bs), BF),
        in_specs=[SMEM, SMEM, VMEM, VMEM, VMEM],
        out_specs=VMEM,
        scratch_shapes=[pltpu.VMEM((rows, groups * bs), BF) for _ in range(2)],
        compiler_params=PARAMS,
        name="pair",
    )(shift, link_ids, masked, borders, scale)
    received = lax.all_to_all(pairs, ("x", "core", "z"), 0, 0, tiled=True)
    bins = pl.pallas_call(
        bin_kernel,
        out_shape=jax.ShapeDtypeStruct((y_count, bins_y, bs, bs), BF),
        in_specs=[HBM],
        out_specs=HBM,
        scratch_shapes=[
            pltpu.VMEM((y_count * bins_y, bs, bs), F32),
            pltpu.VMEM((groups * local_scen, TAG, bs), BF),
            pltpu.VMEM((groups * local_scen, bs, bs), BF),
            pltpu.VMEM((y_count, bins_y, bs, bs), BF),
            pltpu.VMEM((TAG, bs), jnp.int32),
            pltpu.SMEM((TAG, bs), jnp.int32),
            pltpu.SemaphoreType.DMA((groups + 2,)),
            pltpu.SemaphoreType.DMA((y_count,)),
        ],
        compiler_params=WIDE,
        name="bins",
    )(received)
    parts = [lax.all_to_all(bins, "y", 0, 0, tiled=True)]
    place = jnp.stack([tile * group_blocks, z * group_blocks + y * own_cols])
    return pl.pallas_call(
        final_kernel,
        out_shape=jax.ShapeDtypeStruct((group_blocks * bs, own_cols * bs), F32),
        in_specs=[SMEM, VMEM] + [VMEM for _ in parts],
        out_specs=VMEM,
        compiler_params=PARAMS,
        name="final",
    )(place, first_diag.reshape(order_blocks, bs), *parts)


def solution(mesh):
    chips = Mesh(mesh.devices.reshape(8, 4, 4, 2), ("z", "y", "x", "core"))
    scen, tile = ("z", "y"), ("x", "core")
    in_specs = (
        P(scen, None, None),
        P(scen, None, None),
        P(scen, None, tile),
        P(scen, None),
        P(scen, None),
        P(),
    )
    return jax.shard_map(
        on_device, mesh=chips, in_specs=in_specs, out_specs=P(tile, scen), check_vma=False
    )
```

time: 142 us -> 131 us (0.923)
  starting transfers between devices: 18.9 us -> 8.89 us
  Pallas kernels: 8.07 us -> 11.3 us
  blocking collectives: 66.8 us -> 65 us
    all_gather x1 -> x0, blocking collectives: 66.8 us -> none  [on_device(): links = lax.all_gather(link_ids, 'z', axis=0, tiled=True)]
    all_to_all x0 -> x1, blocking collectives: none -> 65 us  [on_device(): received = lax.all_to_all(pairs, ('x', 'core', 'z'), 0, 0, tiled=True)]
    all_to_all x2 -> x1, starting transfers between devices: 14.5 us -> 4.46 us  [on_device(): parts = [lax.all_to_all(bins, 'y', 0, 0, tiled=True)]]
    all_to_all x1, waiting for transfers between devices: 21.3 us -> 15.1 us  [on_device(): borders = lax.all_to_all(border, ('x', 'core'), 0, 0, tiled=True)]
    all_to_all x2 -> x1, waiting for transfers between devices: 20.9 us -> 25.9 us  [on_device(): parts = [lax.all_to_all(bins, 'y', 0, 0, tiled=True)]]
    pallas_call x1 -> x2, Pallas kernels: 1.66 us -> 6.13 us  [the longest x1 3.75 us: on_device(): pl.pallas_call(bin_kernel, out_shape=jax.ShapeDtypeStruct((y_count, bins_...]
    unnamed x13 -> x11, local copies, waits for them, and re-layouts: 5.05 us -> 3.71 us
  transfers between devices with their start and end apart: 3 -> 2, of which waited for: 2 -> 2; matrix products, arithmetic and copies ran while one was open for 0% -> 0% of each run, Pallas kernels for 0% -> 2%
where the time goes in v2:
time: 131 us; the launch traced here: 130 us
  blocking collectives  65 us (50%)
  waiting for transfers between devices  41 us (31%)
  Pallas kernels  11.3 us (9%)
  starting transfers between devices  8.89 us (7%)
  local copies, waits for them, and re-layouts  3.97 us (3%)
    all_to_all x1, blocking collectives, on_device(): received = lax.all_to_all(pairs, ('x', 'core', 'z'), 0, 0, tiled=True)  65 us
    all_to_all x1, waiting for transfers between devices, on_device(): parts = [lax.all_to_all(bins, 'y', 0, 0, tiled=True)]  25.9 us
    all_to_all x1, waiting for transfers between devices, on_device(): borders = lax.all_to_all(border, ('x', 'core'), 0, 0, tiled=True)  15.1 us
    all_to_all x1, starting transfers between devices, on_device(): parts = [lax.all_to_all(bins, 'y', 0, 0, tiled=True)]  4.46 us
    all_to_all x1, starting transfers between devices, on_device(): borders = lax.all_to_all(border, ('x', 'core'), 0, 0, tiled=True)  4.43 us
    pallas_call x1, Pallas kernels, on_device(): pl.pallas_call(bin_kernel, out_shape=jax.ShapeDtypeStruct((y_count, bins_...  3.75 us
    unnamed x11, local copies, waits for them, and re-layouts  3.71 us
    pallas_call x1, Pallas kernels, on_device(): pl.pallas_call(pair_kernel, out_shape=jax.ShapeDtypeStruct((groups * grou...  3.3 us
  transfers between devices with their start and end apart: 2, of which 2 were waited for; matrix products, arithmetic and copies ran while one was open for 0% of the time, Pallas kernels for 2%

profile of v2, /device:TPU:32, one launch (start us, length us, event | category | flops | bytes accessed | tf_op | source)
XLA Modules:
  0.0 130.4 jit_solution(1295557355832124961)
XLA Ops:
  0.0 0.0 copy-start
  0.0 0.0 copy-start.4
  0.0 4.4 %all-to-all-start = ((bf16[8,768,128]{2,1,0:T(8,128)(2,1)}), bf16[8,768,128]{2,1,0:T(8,128)(2,1)S(1)}, u32[]{:S(2)}, u32[]{:S(2)}) async-start(bf16[8,768,128]{2,1,0:T(8,128)(2,1)} %param.8), calls=%async_computation | async-start | bytes 3145728 | tf_op jit(solution)/shard_map/all_to_all | solution.py:162
  4.4 0.0 copy-done.4
  4.5 0.1 reshape.11.pattern_ref
  4.5 0.0 copy-done
  4.5 0.2 copy.9.scale_ref
  4.7 0.0 copy-start.1
  4.7 3.7 %copy-done.1 = bf16[8,768,768]{2,1,0:T(8,128)(2,1)S(1)} copy-done((bf16[8,768,768]{2,1,0:T(8,128)(2,1)S(1)}, bf16[8,768,768]{2,1,0:T(8,128)(2,1)}, u32[]{:S(2)}) %copy-start.1) | copy-done | bytes 9437208
  8.4 0.0 copy-start.3
  8.4 2.4 %mask.1.masked_ref = bf16[768,768]{1,0:T(8,128)(2,1)S(1)} custom-call(s32[1]{0:T(128)} %bitcast.3.tile_ref, s32[8,36]{1,0:T(8,128)S(1)} %reshape.11.pattern_ref, bf16[8,768,768]{2,1,0:T(8,128)(2,1)S(1)} %copy-done.1), custom_call_target="tpu_custom_call" | custom-call | tf_op jit(solution)/shard_map/mask/pallas_call | solution.py:164
  10.8 0.1 pad_add_fusion.1.shift_ref
  10.9 15.1 %all-to-all-done.border_ref = bf16[8,768,128]{2,1,0:T(8,128)(2,1)S(1)} async-done(((bf16[8,768,128]{2,1,0:T(8,128)(2,1)}), bf16[8,768,128]{2,1,0:T(8,128)(2,1)S(1)}, u32[]{:S(2)}, u32[]{:S(2)}) %all-to-all-start) | async-done | bytes 1572896 | tf_op jit(solution)/shard_map/all_to_all | solution.py:162
  26.0 0.0 copy-done.3
  26.0 3.3 %pair.1 = bf16[64,136,128]{2,1,0:T(8,128)(2,1)S(1)} custom-call(s32[4]{0:T(128)S(1)} %pad_add_fusion.1.shift_ref, s32[8,8]{1,0:T(8,128)S(1)} %copy-done.3, bf16[768,768]{1,0:T(8,128)(2,1)S(1)} %mask.1.masked_ref, bf16[8,768,128]{2,1,0:T(8,128)(2,1)S(1)} %all-to-all-done.border_ref, f32[768,1]{1,0:T(8,128)S(1)} %copy.9.scale_ref), custom_call_target="tpu_custom_call" | custom-call | tf_op jit(solution)/shard_map/pair/pallas_call | solution.py:175
  29.3 65.0 %all_to_all.15.blocks_hbm = bf16[64,136,128]{2,1,0:T(8,128)(2,1)} all-to-all(bf16[64,136,128]{2,1,0:T(8,128)(2,1)S(1)} %pair.1), channel_id=1, replica_groups=mesh['z'=8,'y'=4,'x'=4,'core'=2] {'x','core','z'}, dimensions={0} | all-to-all | bytes 4456448 | tf_op jit(solution)/shard_map/all_to_all | solution.py:184
  94.3 3.8 %bins.1 = bf16[4,16,128,128]{3,2,1,0:T(8,128)(2,1)} custom-call(bf16[64,136,128]{2,1,0:T(8,128)(2,1)} %all_to_all.15.blocks_hbm), custom_call_target="tpu_custom_call" | custom-call | tf_op jit(solution)/shard_map/bins/pallas_call | solution.py:185
  98.1 0.0 copy-start.2
  98.1 4.5 %all-to-all-start.2 = ((bf16[4,16,128,128]{3,2,1,0:T(8,128)(2,1)}), bf16[4,16,128,128]{3,2,1,0:T(8,128)(2,1)S(1)}, u32[]{:S(2)}, u32[]{:S(2)}) async-start(bf16[4,16,128,128]{3,2,1,0:T(8,128)(2,1)} %bins.1), calls=%async_computation.2 | async-start | bytes 4194304 | tf_op jit(solution)/shard_map/all_to_all | solution.py:203
  102.6 0.1 pad_add_fusion.where_ref
  102.7 25.9 %all-to-all-done.2.rest_0_ = bf16[4,16,128,128]{3,2,1,0:T(8,128)(2,1)S(1)} async-done(((bf16[4,16,128,128]{3,2,1,0:T(8,128)(2,1)}), bf16[4,16,128,128]{3,2,1,0:T(8,128)(2,1)S(1)}, u32[]{:S(2)}, u32[]{:S(2)}) %all-to-all-start.2) | async-done | bytes 2097184 | tf_op jit(solution)/shard_map/all_to_all | solution.py:203
  128.5 0.0 copy-done.2
  128.6 1.8 %final.1 = f32[1024,256]{1,0:T(8,128)} custom-call(s32[2]{0:T(128)S(1)} %pad_add_fusion.where_ref, f32[64,128]{1,0:T(8,128)S(1)} %bitcast.6, bf16[4,16,128,128]{3,2,1,0:T(8,128)(2,1)S(1)} %all-to-all-done.2.rest_0_), custom_call_target="tpu_custom_call" | custom-call | tf_op jit(solution)/shard_map/final/pallas_call | solution.py:205
  (2 shorter events, 0.0 us)
Async XLA Ops:
  0.0 4.5 %copy-start = (f32[8,768]{1,0:T(8,128)S(1)}, f32[8,768]{1,0:T(8,128)}, u32[]{:S(2)}) copy-start(f32[8,768]{1,0:T(8,128)} %param.9) | copy-start | bytes 73732
  0.0 4.4 %copy-start.4 = (s32[8,6,6]{2,0,1:T(8,128)S(1)}, s32[8,6,6]{2,0,1:T(8,128)}, u32[]{:S(2)}) copy-start(s32[8,6,6]{2,0,1:T(8,128)} %param.7) | copy-start | bytes 3460
  0.0 26.0 %all-to-all-start = ((bf16[8,768,128]{2,1,0:T(8,128)(2,1)}), bf16[8,768,128]{2,1,0:T(8,128)(2,1)S(1)}, u32[]{:S(2)}, u32[]{:S(2)}) async-start(bf16[8,768,128]{2,1,0:T(8,128)(2,1)} %param.8), calls=%async_computation | async-start | bytes 3145728 | tf_op jit(solution)/shard_map/all_to_all | solution.py:162
  4.7 3.7 %copy-start.1 = (bf16[8,768,768]{2,1,0:T(8,128)(2,1)S(1)}, bf16[8,768,768]{2,1,0:T(8,128)(2,1)}, u32[]{:S(2)}) copy-start(bf16[8,768,768]{2,1,0:T(8,128)(2,1)} %factor_hbm.1) | copy-start | bytes 28311556
  8.4 17.6 %copy-start.3 = (s32[8,8]{1,0:T(8,128)S(1)}, s32[8,8]{1,0:T(8,128)}, u32[]{:S(2)}) copy-start(s32[8,8]{1,0:T(8,128)} %link_ref.1) | copy-start | bytes 772
  98.1 30.4 %copy-start.2 = (f32[8192]{0:T(1024)S(1)}, f32[8192]{0:T(1024)}, u32[]{:S(2)}) copy-start(f32[8192]{0:T(1024)} %param.11) | copy-start | bytes 98308
  98.1 30.4 %all-to-all-start.2 = ((bf16[4,16,128,128]{3,2,1,0:T(8,128)(2,1)}), bf16[4,16,128,128]{3,2,1,0:T(8,128)(2,1)S(1)}, u32[]{:S(2)}, u32[]{:S(2)}) async-start(bf16[4,16,128,128]{3,2,1,0:T(8,128)(2,1)} %bins.1), calls=%async_computation.2 | async-start | bytes 4194304 | tf_op jit(solution)/shard_map/all_to_all | solution.py:203

commit v3 on v2

v3 whole, which is shorter than its diff:
```python
import jax
import jax.numpy as jnp
from jax import lax
from jax.experimental import pallas as pl
from jax.experimental.pallas import tpu as pltpu
from jax.sharding import Mesh, PartitionSpec as P

BF = jnp.bfloat16
F32 = jnp.float32
TAG = 8

VMEM = pl.BlockSpec(memory_space=pltpu.VMEM)
SMEM = pl.BlockSpec(memory_space=pltpu.SMEM)
HBM = pl.BlockSpec(memory_space=pltpu.HBM)
PARAMS = pltpu.CompilerParams(vmem_limit_bytes=32 << 20)


def mask_kernel(tile_ref, pattern_ref, factor_hbm, out_ref, buf_ref, sems):
    rows = buf_ref.shape[0]
    nblk = sems.shape[0]
    bs = rows // nblk
    tile = tile_ref[0]
    copies = [
        pltpu.make_async_copy(
            factor_hbm.at[tile, pl.ds(a * bs, bs), :], buf_ref.at[pl.ds(a * bs, bs), :], sems.at[a]
        )
        for a in range(nblk)
    ]
    for copy in copies:
        copy.start()
    for a in range(nblk):
        copies[a].wait()
        lo, hi = a * bs, (a + 1) * bs
        for b in range(nblk):
            block = buf_ref[lo:hi, b * bs:(b + 1) * bs]
            if b < a:
                keep = pattern_ref[tile, a * nblk + b] != 0
                block = jnp.where(keep, block, jnp.zeros_like(block))
            if b > a:
                block = jnp.zeros_like(block)
            out_ref[lo:hi, b * bs:(b + 1) * bs] = block


def pair_kernel(shift_ref, link_ref, masked_ref, border_ref, scale_ref, out_hbm, out_ref, solved_ref, scaled_ref, sems):
    groups, rows, bs = border_ref.shape
    tile, own_cols, bins_y, group_blocks = (shift_ref[k] for k in range(4))
    for g in range(0, groups, 2):
        rhs = jnp.concatenate([border_ref[g], border_ref[g + 1]], axis=1)
        for a in range(0, rows, 2 * bs):
            lo, hi = a, a + 2 * bs
            solved = jnp.dot(
                masked_ref[lo:hi, :hi], rhs[:hi], preferred_element_type=F32
            ).astype(BF)
            solved_ref[lo:hi, g * bs:(g + 2) * bs] = solved
            scaled_ref[lo:hi, g * bs:(g + 2) * bs] = (
                scale_ref[lo:hi, :] * solved.astype(F32)
            ).astype(BF)
    for i in range(groups):
        row_bin = link_ref[tile, i] - i * group_blocks
        for j in range(groups):
            col_bin = link_ref[tile, j] - j * group_blocks
            owner = lax.div(col_bin, own_cols)
            target = owner * bins_y + row_bin * own_cols + (col_bin - owner * own_cols)
            out_ref[i * groups + j, bs:, :] = jnp.full((TAG, bs), target.astype(F32)).astype(BF)
    stores = []
    for i in range(0, groups, 2):
        lhs = scaled_ref[:, i * bs:(i + 2) * bs]
        for j in range(0, groups, 2):
            rhs = solved_ref[:, j * bs:(j + 2) * bs]
            pair = lax.dot_general(
                lhs, rhs, (((0,), (0,)), ((), ())), preferred_element_type=F32
            ).astype(BF)
            for di in range(2):
                for dj in range(2):
                    out_ref[(i + di) * groups + j + dj, :bs, :] = pair[
                        di * bs:(di + 1) * bs, dj * bs:(dj + 1) * bs
                    ]
        part = pl.ds(i * groups, 2 * groups)
        store = pltpu.make_async_copy(out_ref.at[part], out_hbm.at[part], sems.at[i // 2])
        store.start()
        stores.append(store)
    for store in stores:
        store.wait()


def bin_kernel(shift_ref, in_ref, *rest):
    own, far_a, far_b, up_b, down_a, up_a, down_b = rest[:7]
    acc_ref, meta_ref, target_ref, sem = rest[7:]
    count, bs = in_ref.shape[0], in_ref.shape[2]
    lane = lax.broadcasted_iota(jnp.int32, (TAG, bs), 1)
    meta = jnp.zeros((TAG, bs), F32)
    for k in range(count):
        meta = jnp.where(lane == k, in_ref[k, bs:, :].astype(F32), meta)
    meta_ref[...] = meta.astype(jnp.int32)
    targets = pltpu.make_async_copy(meta_ref, target_ref, sem)
    targets.start()
    acc_ref[...] = jnp.zeros_like(acc_ref)
    targets.wait()
    for k in range(count):
        acc_ref[target_ref[0, k]] += in_ref[k, :bs, :].astype(F32)
    per = own.shape[0]
    parts = acc_ref.shape[0] // per
    for hop, pieces in ((2, (far_a, far_b)), (1, (up_a, up_b)), (3, (down_a, down_b)), (0, (own,))):
        start = lax.rem(shift_ref[0] + hop, parts) * per
        size = per // len(pieces)
        for n, piece in enumerate(pieces):
            piece[...] = acc_ref[pl.ds(start + n * size, size)].astype(BF)


def final_kernel(where_ref, diag_ref, own_ref, up_a_ref, down_a_ref, up_b_ref, down_b_ref, out_ref):
    count, bs, _ = own_ref.shape
    row_blocks = out_ref.shape[0] // bs
    col_blocks = out_ref.shape[1] // bs
    half = count // 2
    first_row = where_ref[0]
    first_col = where_ref[1]
    eye = lax.broadcasted_iota(jnp.int32, (bs, bs), 0) == lax.broadcasted_iota(jnp.int32, (bs, bs), 1)
    for r in range(row_blocks):
        diag = diag_ref[pl.ds(first_row + r, 1), :]
        for c in range(col_blocks):
            n = r * col_blocks + c
            one, two = (up_a_ref, down_a_ref) if n < half else (up_b_ref, down_b_ref)
            total = own_ref[n].astype(F32) + one[n % half].astype(F32) + two[n % half].astype(F32)
            on = jnp.logical_and(eye, first_row + r == first_col + c)
            total = total + jnp.where(on, jnp.broadcast_to(diag, (bs, bs)), 0.0)
            out_ref[r * bs:(r + 1) * bs, c * bs:(c + 1) * bs] = total


def on_device(factor_inv, pattern, border, row_scale, link_ids, first_diag):
    local_scen, rows, _ = factor_inv.shape
    nblk = pattern.shape[1]
    bs = border.shape[2]
    groups = link_ids.shape[1]
    tile = lax.axis_index(("x", "core"))
    z = lax.axis_index("z")
    y = lax.axis_index("y")
    y_count = lax.axis_size("y")
    order_blocks = first_diag.shape[0] // bs
    group_blocks = order_blocks // groups
    own_cols = group_blocks // y_count
    bins_y = group_blocks * own_cols

    borders = lax.all_to_all(border, ("x", "core"), 0, 0, tiled=True)

    masked = pl.pallas_call(
        mask_kernel,
        out_shape=jax.ShapeDtypeStruct((rows, rows), BF),
        in_specs=[SMEM, SMEM, HBM],
        out_specs=VMEM,
        scratch_shapes=[pltpu.VMEM((rows, rows), BF), pltpu.SemaphoreType.DMA((nblk,))],
        compiler_params=PARAMS,
        name="mask",
    )(tile.reshape(1), pattern.reshape(local_scen, nblk * nblk), factor_inv)
    scale = lax.dynamic_slice_in_dim(row_scale, tile, 1, 0).reshape(rows, 1)
    shift = jnp.stack([tile, jnp.int32(own_cols), jnp.int32(bins_y), jnp.int32(group_blocks)])
    pairs = pl.pallas_call(
        pair_kernel,
        out_shape=jax.ShapeDtypeStruct((groups * groups, bs + TAG, bs), BF),
        in_specs=[SMEM, SMEM, VMEM, VMEM, VMEM],
        out_specs=HBM,
        scratch_shapes=[pltpu.VMEM((groups * groups, bs + TAG, bs), BF)]
        + [pltpu.VMEM((rows, groups * bs), BF) for _ in range(2)]
        + [pltpu.SemaphoreType.DMA((groups // 2,))],
        compiler_params=PARAMS,
        name="pair",
    )(shift, link_ids, masked, borders, scale)
    received = lax.all_to_all(pairs, ("x", "core", "z"), 0, 0, tiled=True)
    half = jax.ShapeDtypeStruct((bins_y // 2, bs, bs), BF)
    own, far_a, far_b, up_b, down_a, up_a, down_b = pl.pallas_call(
        bin_kernel,
        out_shape=[jax.ShapeDtypeStruct((bins_y, bs, bs), BF)] + [half] * 6,
        in_specs=[SMEM, VMEM],
        out_specs=[VMEM] * 7,
        scratch_shapes=[
            pltpu.VMEM((y_count * bins_y, bs, bs), F32),
            pltpu.VMEM((TAG, bs), jnp.int32),
            pltpu.SMEM((TAG, bs), jnp.int32),
            pltpu.SemaphoreType.DMA,
        ],
        compiler_params=PARAMS,
        name="bins",
    )(y.reshape(1), received)
    def send(value, hop):
        return lax.ppermute(value, "y", [(k, (k + hop) % y_count) for k in range(y_count)])

    def add(one, two):
        return (one.astype(F32) + two.astype(F32)).astype(BF)

    far_a, far_b = send(far_a, 1), send(far_b, -1)
    up_b, down_a = send(up_b, 1), send(down_a, -1)
    up_a, down_b = send(add(up_a, far_a), 1), send(add(down_b, far_b), -1)
    place = jnp.stack([tile * group_blocks, z * group_blocks + y * own_cols])
    return pl.pallas_call(
        final_kernel,
        out_shape=jax.ShapeDtypeStruct((group_blocks * bs, own_cols * bs), F32),
        in_specs=[SMEM] + [VMEM] * 6,
        out_specs=VMEM,
        compiler_params=PARAMS,
        name="final",
    )(place, first_diag.reshape(order_blocks, bs), own, up_a, down_a, up_b, down_b)


def solution(mesh):
    chips = Mesh(mesh.devices.reshape(8, 4, 4, 2), ("z", "y", "x", "core"))
    scen, tile = ("z", "y"), ("x", "core")
    in_specs = (
        P(scen, None, None),
        P(scen, None, None),
        P(scen, None, tile),
        P(scen, None),
        P(scen, None),
        P(),
    )
    return jax.shard_map(
        on_device, mesh=chips, in_specs=in_specs, out_specs=P(tile, scen), check_vma=False
    )
```

time: 131 us -> 119 us (0.908)
  blocking collectives: 65 us -> 0 us
  waiting for transfers between devices: 41 us -> 80 us
  starting transfers between devices: 8.89 us -> 23.1 us
  Pallas kernels: 11.3 us -> 9.87 us
    all_to_all x1 -> x0, blocking collectives: 65 us -> none  [on_device(): received = lax.all_to_all(pairs, ('x', 'core', 'z'), 0, 0, tiled=True)]
    all_to_all x1, waiting for transfers between devices: 25.9 us -> 54 us  [on_device(): received = lax.all_to_all(pairs, ('x', 'core', 'z'), 0, 0, tiled=True)]
    ppermute x0 -> x6, waiting for transfers between devices: none -> 10.9 us  [send(): lax.ppermute(value, 'y', [(k, (k + hop) % y_count) for k in range(y_count)])]
    ppermute x0 -> x6, starting transfers between devices: none -> 8.91 us  [send(): lax.ppermute(value, 'y', [(k, (k + hop) % y_count) for k in range(y_count)])]
    all_to_all x1, starting transfers between devices: 4.46 us -> 9.74 us  [on_device(): received = lax.all_to_all(pairs, ('x', 'core', 'z'), 0, 0, tiled=True)]
    pallas_call x1, Pallas kernels: 3.75 us -> 1.55 us  [on_device(): pl.pallas_call(bin_kernel, out_shape=[jax.ShapeDtypeStruct((bins_y, bs, b...]
  transfers between devices with their start and end apart: 2 -> 8, of which waited for: 2 -> 5; matrix products, arithmetic and copies ran while one was open for 0% -> 0% of each run, Pallas kernels for 2% -> 2%
where the time goes in v3:
time: 119 us; the launch traced here: 117 us
  waiting for transfers between devices  80 us (67%)
  starting transfers between devices  23.1 us (19%)
  Pallas kernels  9.87 us (8%)
  local copies, waits for them, and re-layouts  3.97 us (3%)
    all_to_all x1, waiting for transfers between devices, on_device(): received = lax.all_to_all(pairs, ('x', 'core', 'z'), 0, 0, tiled=True)  54 us
    all_to_all x1, waiting for transfers between devices, on_device(): borders = lax.all_to_all(border, ('x', 'core'), 0, 0, tiled=True)  15.1 us
    ppermute x6, waiting for transfers between devices, send(): lax.ppermute(value, 'y', [(k, (k + hop) % y_count) for k in range(y_count)])  10.9 us
    all_to_all x1, starting transfers between devices, on_device(): received = lax.all_to_all(pairs, ('x', 'core', 'z'), 0, 0, tiled=True)  9.74 us
    ppermute x6, starting transfers between devices, send(): lax.ppermute(value, 'y', [(k, (k + hop) % y_count) for k in range(y_count)])  8.91 us
    all_to_all x1, starting transfers between devices, on_device(): borders = lax.all_to_all(border, ('x', 'core'), 0, 0, tiled=True)  4.43 us
    pallas_call x1, Pallas kernels, on_device(): pl.pallas_call(pair_kernel, out_shape=jax.ShapeDtypeStruct((groups * grou...  4.18 us
    unnamed x11, local copies, waits for them, and re-layouts  3.71 us
  transfers between devices with their start and end apart: 8, of which 5 were waited for; matrix products, arithmetic and copies ran while one was open for 0% of the time, Pallas kernels for 2%

profile of v3, /device:TPU:32, one launch (start us, length us, event | category | flops | bytes accessed | tf_op | source)
XLA Modules:
  0.0 117.3 jit_solution(17425574294160066640)
XLA Ops:
  0.0 0.0 copy-start
  0.0 4.4 %all-to-all-start = ((bf16[8,768,128]{2,1,0:T(8,128)(2,1)}), bf16[8,768,128]{2,1,0:T(8,128)(2,1)S(1)}, u32[]{:S(2)}, u32[]{:S(2)}) async-start(bf16[8,768,128]{2,1,0:T(8,128)(2,1)} %param.8), calls=%async_computation | async-start | bytes 3145728 | tf_op jit(solution)/shard_map/all_to_all | solution.py:143
  4.4 0.0 copy-done.4
  4.5 0.1 reshape.15.pattern_ref
  4.5 0.2 copy.9.scale_ref
  4.7 0.0 copy-start.1
  4.7 3.7 %copy-done.1 = bf16[8,768,768]{2,1,0:T(8,128)(2,1)S(1)} copy-done((bf16[8,768,768]{2,1,0:T(8,128)(2,1)S(1)}, bf16[8,768,768]{2,1,0:T(8,128)(2,1)}, u32[]{:S(2)}) %copy-start.1) | copy-done | bytes 9437208
  8.4 2.4 %mask.1.masked_ref = bf16[768,768]{1,0:T(8,128)(2,1)S(1)} custom-call(s32[1]{0:T(128)} %bitcast.4.tile_ref, s32[8,36]{1,0:T(8,128)S(1)} %reshape.15.pattern_ref, bf16[8,768,768]{2,1,0:T(8,128)(2,1)S(1)} %copy-done.1), custom_call_target="tpu_custom_call" | custom-call | tf_op jit(solution)/shard_map/mask/pallas_call | solution.py:145
  10.8 0.1 pad_add_fusion.1.shift_ref
  10.9 15.1 %all-to-all-done.border_ref = bf16[8,768,128]{2,1,0:T(8,128)(2,1)S(1)} async-done(((bf16[8,768,128]{2,1,0:T(8,128)(2,1)}), bf16[8,768,128]{2,1,0:T(8,128)(2,1)S(1)}, u32[]{:S(2)}, u32[]{:S(2)}) %all-to-all-start) | async-done | bytes 1572896 | tf_op jit(solution)/shard_map/all_to_all | solution.py:143
  26.0 4.2 %pair.1 = bf16[64,136,128]{2,1,0:T(8,128)(2,1)} custom-call(s32[4]{0:T(128)S(1)} %pad_add_fusion.1.shift_ref, s32[8,8]{1,0:T(8,128)S(1)} %copy-done.3, bf16[768,768]{1,0:T(8,128)(2,1)S(1)} %mask.1.masked_ref, bf16[8,768,128]{2,1,0:T(8,128)(2,1)S(1)} %all-to-all-done.border_ref, f32[768,1]{1,0:T(8,128)S(1)} %copy.9.scale_ref), custom_call_target="tpu_custom_call" | custom-call | tf_op jit(solution)/shard_map/pair/pallas_call | solution.py:156
  30.2 9.7 %all-to-all-start.1 = ((bf16[64,136,128]{2,1,0:T(8,128)(2,1)}), bf16[64,136,128]{2,1,0:T(8,128)(2,1)S(1)}, u32[]{:S(2)}, u32[]{:S(2)}) async-start(bf16[64,136,128]{2,1,0:T(8,128)(2,1)} %pair.1), calls=%async_computation.1 | async-start | bytes 4456448 | tf_op jit(solution)/shard_map/all_to_all | solution.py:167
  40.0 0.0 copy-start.2
  40.0 54.0 %all-to-all-done.1.in_ref = bf16[64,136,128]{2,1,0:T(8,128)(2,1)S(1)} async-done(((bf16[64,136,128]{2,1,0:T(8,128)(2,1)}), bf16[64,136,128]{2,1,0:T(8,128)(2,1)S(1)}, u32[]{:S(2)}, u32[]{:S(2)}) %all-to-all-start.1) | async-done | bytes 2228256 | tf_op jit(solution)/shard_map/all_to_all | solution.py:167
  94.0 1.5 %bins.1 = (bf16[16,128,128]{2,1,0:T(8,128)(2,1)S(1)}, bf16[8,128,128]{2,1,0:T(8,128)(2,1)S(1)}, bf16[8,128,128]{2,1,0:T(8,128)(2,1)S(1)}, bf16[8,128,128]{2,1,0:...) custom-call(s32[1]{0:T(128)} %bitcast.3.shift_ref, ...), custom_call_target="tpu_custom_call" | custom-call | tf_op jit(solution)/shard_map/bins/pallas_call | solution.py:169
  95.5 1.7 %collective-permute-start = (bf16[8,128,128]{2,1,0:T(8,128)(2,1)S(1)}, bf16[8,128,128]{2,1,0:T(8,128)(2,1)S(1)}, u32[]{:S(2)}, u32[]{:S(2)}) collective-permute-start(bf16[8,128,128]{2,1,0:T(8,128)(2,1)S(1)} %get-tuple-element.14), channel_id=1, source_target_pairs={{0,8},{8,16},{16,24},{24,0},{1,9},{9,17},{17,25},{25,1},{2,10},{10... | collective-permute-start | bytes 786440 | tf_op jit(solution)/shard_map/ppermute | solution.py:184
  97.2 1.7 %collective-permute-start.4 = (bf16[8,128,128]{2,1,0:T(8,128)(2,1)S(1)}, bf16[8,128,128]{2,1,0:T(8,128)(2,1)S(1)}, u32[]{:S(2)}, u32[]{:S(2)}) collective-permute-start(bf16[8,128,128]{2,1,0:T(8,128)(2,1)S(1)} %get-tuple-element.18), channel_id=1, source_target_pairs={{0,24},{8,0},{16,8},{24,16},{1,25},{9,1},{17,9},{25,17},{2,26},{10... | collective-permute-start | bytes 786440 | tf_op jit(solution)/shard_map/ppermute | solution.py:184
  98.8 1.8 %collective-permute-start.2 = (bf16[8,128,128]{2,1,0:T(8,128)(2,1)S(1)}, bf16[8,128,128]{2,1,0:T(8,128)(2,1)S(1)}, u32[]{:S(2)}, u32[]{:S(2)}) collective-permute-start(bf16[8,128,128]{2,1,0:T(8,128)(2,1)S(1)} %get-tuple-element.15), channel_id=1, source_target_pairs={{0,24},{8,0},{16,8},{24,16},{1,25},{9,1},{17,9},{25,17},{2,26},{10... | collective-permute-start | bytes 786440 | tf_op jit(solution)/shard_map/ppermute | solution.py:184
  100.6 0.2 collective-permute-start.3
  100.9 4.9 %collective-permute-done = bf16[8,128,128]{2,1,0:T(8,128)(2,1)S(1)} collective-permute-done((bf16[8,128,128]{2,1,0:T(8,128)(2,1)S(1)}, bf16[8,128,128]{2,1,0:T(8,128)(2,1)S(1)}, u32[]{:S(2)}, u32[]{:S(2)}) %collective-permute-start) | collective-permute-done | bytes 262176 | tf_op jit(solution)/shard_map/ppermute | solution.py:184
  105.7 0.1 add_convert_fusion.1
  105.8 0.8 collective-permute-start.1
  106.6 0.0 collective-permute-done.4
  106.6 0.1 add_convert_fusion
  106.7 2.8 %collective-permute-start.5 = (bf16[8,128,128]{2,1,0:T(8,128)(2,1)S(1)}, bf16[8,128,128]{2,1,0:T(8,128)(2,1)S(1)}, u32[]{:S(2)}, u32[]{:S(2)}) collective-permute-start(bf16[8,128,128]{2,1,0:T(8,128)(2,1)S(1)} %add_convert_fusion), channel_id=1, source_target_pairs={{0,24},{8,0},{16,8},{24,16},{1,25},{9,1},{17,9},{25,17},{2,26},{10... | collective-permute-start | bytes 786440 | tf_op jit(solution)/shard_map/ppermute | solution.py:184
  109.5 0.1 pad_add_fusion.where_ref
  109.5 2.5 %collective-permute-done.2.down_a_ref = bf16[8,128,128]{2,1,0:T(8,128)(2,1)S(1)} collective-permute-done((bf16[8,128,128]{2,1,0:T(8,128)(2,1)S(1)}, bf16[8,128,128]{2,1,0:T(8,128)(2,1)S(1)}, u32[]{:S(2)}, u32[]{:S(2)}) %collective-permute-start.2) | collective-permute-done | bytes 262176 | tf_op jit(solution)/shard_map/ppermute | solution.py:184
  112.1 0.0 collective-permute-done.3.up_b_ref
  112.1 3.5 %collective-permute-done.1.up_a_ref = bf16[8,128,128]{2,1,0:T(8,128)(2,1)S(1)} collective-permute-done((bf16[8,128,128]{2,1,0:T(8,128)(2,1)S(1)}, bf16[8,128,128]{2,1,0:T(8,128)(2,1)S(1)}, u32[]{:S(2)}, u32[]{:S(2)}) %collective-permute-start.1) | collective-permute-done | bytes 262176 | tf_op jit(solution)/shard_map/ppermute | solution.py:184
  115.6 0.0 collective-permute-done.5.down_b_ref
  115.6 0.0 copy-done.2
  115.6 1.8 %final.1 = f32[1024,256]{1,0:T(8,128)} custom-call(s32[2]{0:T(128)S(1)} %pad_add_fusion.where_ref, f32[64,128]{1,0:T(8,128)S(1)} %bitcast.7, bf16[16,128,128]{2,1,0:T(8,128)(2,1)S(1)} %get-tuple-element.12.own_ref, bf16[8,128,128]{2,1,0:T(8,128)(2,1)S(1)} %collective-permute-done.1.up_a_ref, bf16[8,128,128]{2,1,0:T(8,128)(2,1)S(1)} %collective-permute-done.2.down_a_ref, ...), custom_call_target="tpu_custom_call" | custom-call | tf_op jit(solution)/shard_map/final/pallas_call | solution.py:193
  (6 shorter events, 0.0 us)
Async XLA Ops:
  0.0 4.5 %copy-start = (f32[8,768]{1,0:T(8,128)S(1)}, f32[8,768]{1,0:T(8,128)}, u32[]{:S(2)}) copy-start(f32[8,768]{1,0:T(8,128)} %param.9) | copy-start | bytes 73732
  0.0 4.4 %copy-start.4 = (s32[8,6,6]{2,0,1:T(8,128)S(1)}, s32[8,6,6]{2,0,1:T(8,128)}, u32[]{:S(2)}) copy-start(s32[8,6,6]{2,0,1:T(8,128)} %param.7) | copy-start | bytes 3460
  0.0 26.0 %all-to-all-start = ((bf16[8,768,128]{2,1,0:T(8,128)(2,1)}), bf16[8,768,128]{2,1,0:T(8,128)(2,1)S(1)}, u32[]{:S(2)}, u32[]{:S(2)}) async-start(bf16[8,768,128]{2,1,0:T(8,128)(2,1)} %param.8), calls=%async_computation | async-start | bytes 3145728 | tf_op jit(solution)/shard_map/all_to_all | solution.py:143
  4.7 3.7 %copy-start.1 = (bf16[8,768,768]{2,1,0:T(8,128)(2,1)S(1)}, bf16[8,768,768]{2,1,0:T(8,128)(2,1)}, u32[]{:S(2)}) copy-start(bf16[8,768,768]{2,1,0:T(8,128)(2,1)} %factor_hbm.1) | copy-start | bytes 28311556
  8.4 17.6 %copy-start.3 = (s32[8,8]{1,0:T(8,128)S(1)}, s32[8,8]{1,0:T(8,128)}, u32[]{:S(2)}) copy-start(s32[8,8]{1,0:T(8,128)} %link_ref.1) | copy-start | bytes 772
  30.2 63.8 %all-to-all-start.1 = ((bf16[64,136,128]{2,1,0:T(8,128)(2,1)}), bf16[64,136,128]{2,1,0:T(8,128)(2,1)S(1)}, u32[]{:S(2)}, u32[]{:S(2)}) async-start(bf16[64,136,128]{2,1,0:T(8,128)(2,1)} %pair.1), calls=%async_computation.1 | async-start | bytes 4456448 | tf_op jit(solution)/shard_map/all_to_all | solution.py:167
  40.0 75.6 %copy-start.2 = (f32[8192]{0:T(1024)S(1)}, f32[8192]{0:T(1024)}, u32[]{:S(2)}) copy-start(f32[8192]{0:T(1024)} %param.11) | copy-start | bytes 98308
  95.5 10.2 %collective-permute-start = (bf16[8,128,128]{2,1,0:T(8,128)(2,1)S(1)}, bf16[8,128,128]{2,1,0:T(8,128)(2,1)S(1)}, u32[]{:S(2)}, u32[]{:S(2)}) collective-permute-start(bf16[8,128,128]{2,1,0:T(8,128)(2,1)S(1)} %get-tuple-element.14), channel_id=1, source_target_pairs={{0,8},{8,16},{16,24},{24,0},{1,9},{9,17},{17,25},{25,1},{2,10},{10... | collective-permute-start | bytes 786440 | tf_op jit(solution)/shard_map/ppermute | solution.py:184
  97.2 9.4 %collective-permute-start.4 = (bf16[8,128,128]{2,1,0:T(8,128)(2,1)S(1)}, bf16[8,128,128]{2,1,0:T(8,128)(2,1)S(1)}, u32[]{:S(2)}, u32[]{:S(2)}) collective-permute-start(bf16[8,128,128]{2,1,0:T(8,128)(2,1)S(1)} %get-tuple-element.18), channel_id=1, source_target_pairs={{0,24},{8,0},{16,8},{24,16},{1,25},{9,1},{17,9},{25,17},{2,26},{10... | collective-permute-start | bytes 786440 | tf_op jit(solution)/shard_map/ppermute | solution.py:184
  98.8 13.2 %collective-permute-start.2 = (bf16[8,128,128]{2,1,0:T(8,128)(2,1)S(1)}, bf16[8,128,128]{2,1,0:T(8,128)(2,1)S(1)}, u32[]{:S(2)}, u32[]{:S(2)}) collective-permute-start(bf16[8,128,128]{2,1,0:T(8,128)(2,1)S(1)} %get-tuple-element.15), channel_id=1, source_target_pairs={{0,24},{8,0},{16,8},{24,16},{1,25},{9,1},{17,9},{25,17},{2,26},{10... | collective-permute-start | bytes 786440 | tf_op jit(solution)/shard_map/ppermute | solution.py:184
  100.6 11.4 %collective-permute-start.3 = (bf16[8,128,128]{2,1,0:T(8,128)(2,1)S(1)}, bf16[8,128,128]{2,1,0:T(8,128)(2,1)S(1)}, u32[]{:S(2)}, u32[]{:S(2)}) collective-permute-start(bf16[8,128,128]{2,1,0:T(8,128)(2,1)S(1)} %get-tuple-element.16), channel_id=1, source_target_pairs={{0,8},{8,16},{16,24},{24,0},{1,9},{9,17},{17,25},{25,1},{2,10},{10... | collective-permute-start | bytes 786440 | tf_op jit(solution)/shard_map/ppermute | solution.py:184
  105.8 9.7 %collective-permute-start.1 = (bf16[8,128,128]{2,1,0:T(8,128)(2,1)S(1)}, bf16[8,128,128]{2,1,0:T(8,128)(2,1)S(1)}, u32[]{:S(2)}, u32[]{:S(2)}) collective-permute-start(bf16[8,128,128]{2,1,0:T(8,128)(2,1)S(1)} %add_convert_fusion.1), channel_id=1, source_target_pairs={{0,8},{8,16},{16,24},{24,0},{1,9},{9,17},{17,25},{25,1},{2,10},{10... | collective-permute-start | bytes 786440 | tf_op jit(solution)/shard_map/ppermute | solution.py:184
  106.7 8.9 %collective-permute-start.5 = (bf16[8,128,128]{2,1,0:T(8,128)(2,1)S(1)}, bf16[8,128,128]{2,1,0:T(8,128)(2,1)S(1)}, u32[]{:S(2)}, u32[]{:S(2)}) collective-permute-start(bf16[8,128,128]{2,1,0:T(8,128)(2,1)S(1)} %add_convert_fusion), channel_id=1, source_target_pairs={{0,24},{8,0},{16,8},{24,16},{1,25},{9,1},{17,9},{25,17},{2,26},{10... | collective-permute-start | bytes 786440 | tf_op jit(solution)/shard_map/ppermute | solution.py:184

commit v4 on v3

--- a/solution.py
+++ b/solution.py
@@ -7,7 +7,6 @@
 
 BF = jnp.bfloat16
 F32 = jnp.float32
-TAG = 8
 
 VMEM = pl.BlockSpec(memory_space=pltpu.VMEM)
 SMEM = pl.BlockSpec(memory_space=pltpu.SMEM)
@@ -41,9 +40,8 @@
             out_ref[lo:hi, b * bs:(b + 1) * bs] = block
 
 
-def pair_kernel(shift_ref, link_ref, masked_ref, border_ref, scale_ref, out_hbm, out_ref, solved_ref, scaled_ref, sems):
+def pair_kernel(masked_ref, border_ref, scale_ref, out_ref, solved_ref, scaled_ref):
     groups, rows, bs = border_ref.shape
-    tile, own_cols, bins_y, group_blocks = (shift_ref[k] for k in range(4))
     for g in range(0, groups, 2):
         rhs = jnp.concatenate([border_ref[g], border_ref[g + 1]], axis=1)
         for a in range(0, rows, 2 * bs):
@@ -55,14 +53,6 @@
             scaled_ref[lo:hi, g * bs:(g + 2) * bs] = (
                 scale_ref[lo:hi, :] * solved.astype(F32)
             ).astype(BF)
-    for i in range(groups):
-        row_bin = link_ref[tile, i] - i * group_blocks
-        for j in range(groups):
-            col_bin = link_ref[tile, j] - j * group_blocks
-            owner = lax.div(col_bin, own_cols)
-            target = owner * bins_y + row_bin * own_cols + (col_bin - owner * own_cols)
-            out_ref[i * groups + j, bs:, :] = jnp.full((TAG, bs), target.astype(F32)).astype(BF)
-    stores = []
     for i in range(0, groups, 2):
         lhs = scaled_ref[:, i * bs:(i + 2) * bs]
         for j in range(0, groups, 2):
@@ -72,32 +62,17 @@
             ).astype(BF)
             for di in range(2):
                 for dj in range(2):
-                    out_ref[(i + di) * groups + j + dj, :bs, :] = pair[
+                    out_ref[(i + di) * groups + j + dj] = pair[
                         di * bs:(di + 1) * bs, dj * bs:(dj + 1) * bs
                     ]
-        part = pl.ds(i * groups, 2 * groups)
-        store = pltpu.make_async_copy(out_ref.at[part], out_hbm.at[part], sems.at[i // 2])
-        store.start()
-        stores.append(store)
-    for store in stores:
-        store.wait()
 
 
-def bin_kernel(shift_ref, in_ref, *rest):
+def bin_kernel(shift_ref, target_ref, in_ref, *rest):
     own, far_a, far_b, up_b, down_a, up_a, down_b = rest[:7]
-    acc_ref, meta_ref, target_ref, sem = rest[7:]
-    count, bs = in_ref.shape[0], in_ref.shape[2]
-    lane = lax.broadcasted_iota(jnp.int32, (TAG, bs), 1)
-    meta = jnp.zeros((TAG, bs), F32)
-    for k in range(count):
-        meta = jnp.where(lane == k, in_ref[k, bs:, :].astype(F32), meta)
-    meta_ref[...] = meta.astype(jnp.int32)
-    targets = pltpu.make_async_copy(meta_ref, target_ref, sem)
-    targets.start()
+    acc_ref = rest[7]
     acc_ref[...] = jnp.zeros_like(acc_ref)
-    targets.wait()
-    for k in range(count):
-        acc_ref[target_ref[0, k]] += in_ref[k, :bs, :].astype(F32)
+    for k in range(in_ref.shape[0]):
+        acc_ref[target_ref[k]] += in_ref[k].astype(F32)
     per = own.shape[0]
     parts = acc_ref.shape[0] // per
     for hop, pieces in ((2, (far_a, far_b)), (1, (up_a, up_b)), (3, (down_a, down_b)), (0, (own,))):
@@ -152,34 +127,41 @@
         name="mask",
     )(tile.reshape(1), pattern.reshape(local_scen, nblk * nblk), factor_inv)
     scale = lax.dynamic_slice_in_dim(row_scale, tile, 1, 0).reshape(rows, 1)
-    shift = jnp.stack([tile, jnp.int32(own_cols), jnp.int32(bins_y), jnp.int32(group_blocks)])
+    z_count = lax.axis_size("z")
+    links = link_ids[None]
+    step = 1
+    while step < z_count:
+        moved = lax.ppermute(links, "z", [(i, (i + step) % z_count) for i in range(z_count)])
+        links = jnp.concatenate([links, moved])
+        step *= 2
+    links = links[(z - jnp.arange(z_count)) % z_count]
+    row_bin = lax.dynamic_slice_in_dim(links, tile, 1, 2)[:, :, 0] - tile * group_blocks
+    col_bin = lax.dynamic_slice_in_dim(links, z, 1, 2)[:, :, 0] - z * group_blocks
+    target = (col_bin // own_cols) * bins_y + row_bin * own_cols + col_bin % own_cols
+    target = target.T.reshape(-1)
+    borders, masked, scale, target = lax.optimization_barrier((borders, masked, scale, target))
     pairs = pl.pallas_call(
         pair_kernel,
-        out_shape=jax.ShapeDtypeStruct((groups * groups, bs + TAG, bs), BF),
-        in_specs=[SMEM, SMEM, VMEM, VMEM, VMEM],
-        out_specs=HBM,
-        scratch_shapes=[pltpu.VMEM((groups * groups, bs + TAG, bs), BF)]
-        + [pltpu.VMEM((rows, groups * bs), BF) for _ in range(2)]
-        + [pltpu.SemaphoreType.DMA((groups // 2,))],
+        out_shape=jax.ShapeDtypeStruct((groups * groups, bs, bs), BF),
+        in_specs=[VMEM, VMEM, VMEM],
+        out_specs=VMEM,
+        scratch_shapes=[pltpu.VMEM((rows, groups * bs), BF) for _ in range(2)],
         compiler_params=PARAMS,
         name="pair",
-    )(shift, link_ids, masked, borders, scale)
+    )(masked, borders, scale)
     received = lax.all_to_all(pairs, ("x", "core", "z"), 0, 0, tiled=True)
     half = jax.ShapeDtypeStruct((bins_y // 2, bs, bs), BF)
     own, far_a, far_b, up_b, down_a, up_a, down_b = pl.pallas_call(
         bin_kernel,
         out_shape=[jax.ShapeDtypeStruct((bins_y, bs, bs), BF)] + [half] * 6,
-        in_specs=[SMEM, VMEM],
+        in_specs=[SMEM, SMEM, VMEM],
         out_specs=[VMEM] * 7,
         scratch_shapes=[
             pltpu.VMEM((y_count * bins_y, bs, bs), F32),
-            pltpu.VMEM((TAG, bs), jnp.int32),
-            pltpu.SMEM((TAG, bs), jnp.int32),
-            pltpu.SemaphoreType.DMA,
         ],
         compiler_params=PARAMS,
         name="bins",
-    )(y.reshape(1), received)
+    )(y.reshape(1), target, received)
     def send(value, hop):
         return lax.ppermute(value, "y", [(k, (k + hop) % y_count) for k in range(y_count)])
 

time: 119 us -> 117 us (0.983)
  waiting for transfers between devices: 80 us -> 66.8 us
  starting transfers between devices: 23.1 us -> 32.8 us
  local copies, waits for them, and re-layouts: 3.97 us -> 6.01 us
  Pallas kernels: 9.87 us -> 8.28 us
    all_to_all x1, waiting for transfers between devices: 15.1 us -> 0.01 us  [on_device(): borders = lax.all_to_all(border, ('x', 'core'), 0, 0, tiled=True)]
    ppermute x0 -> x3, starting transfers between devices: none -> 11.2 us  [on_device(): lax.ppermute(links, 'z', [(i, (i + step) % z_count) for i in range(z_coun...]
    ppermute x0 -> x3, waiting for transfers between devices: none -> 4.57 us  [on_device(): lax.ppermute(links, 'z', [(i, (i + step) % z_count) for i in range(z_coun...]
    all_to_all x1, waiting for transfers between devices: 54 us -> 51.2 us  [on_device(): received = lax.all_to_all(pairs, ('x', 'core', 'z'), 0, 0, tiled=True)]
    pallas_call x1, Pallas kernels: 4.18 us -> 2.69 us  [on_device(): pl.pallas_call(pair_kernel, out_shape=jax.ShapeDtypeStruct((groups * grou...]
    all_to_all x1, starting transfers between devices: 9.74 us -> 8.31 us  [on_device(): received = lax.all_to_all(pairs, ('x', 'core', 'z'), 0, 0, tiled=True)]
    unnamed x11 -> x13, local copies, waits for them, and re-layouts: 3.71 us -> 5.03 us
  transfers between devices with their start and end apart: 8 -> 11, of which waited for: 5 -> 6; matrix products, arithmetic and copies ran while one was open for 0% -> 1% of each run, Pallas kernels for 2% -> 2%
where the time goes in v4:
time: 117 us; the launch traced here: 115 us
  waiting for transfers between devices  66.8 us (57%)
  starting transfers between devices  32.8 us (28%)
  Pallas kernels  8.28 us (7%)
  local copies, waits for them, and re-layouts  6.01 us (5%)
    all_to_all x1, waiting for transfers between devices, on_device(): received = lax.all_to_all(pairs, ('x', 'core', 'z'), 0, 0, tiled=True)  51.2 us
    ppermute x3, starting transfers between devices, on_device(): lax.ppermute(links, 'z', [(i, (i + step) % z_count) for i in range(z_coun...  11.2 us
    ppermute x6, waiting for transfers between devices, send(): lax.ppermute(value, 'y', [(k, (k + hop) % y_count) for k in range(y_count)])  11.1 us
    ppermute x6, starting transfers between devices, send(): lax.ppermute(value, 'y', [(k, (k + hop) % y_count) for k in range(y_count)])  8.81 us
    all_to_all x1, starting transfers between devices, on_device(): received = lax.all_to_all(pairs, ('x', 'core', 'z'), 0, 0, tiled=True)  8.31 us
    unnamed x13, local copies, waits for them, and re-layouts  5.03 us
    ppermute x3, waiting for transfers between devices, on_device(): lax.ppermute(links, 'z', [(i, (i + step) % z_count) for i in range(z_coun...  4.57 us
    all_to_all x1, starting transfers between devices, on_device(): borders = lax.all_to_all(border, ('x', 'core'), 0, 0, tiled=True)  4.44 us
  transfers between devices with their start and end apart: 11, of which 6 were waited for; matrix products, arithmetic and copies ran while one was open for 1% of the time, Pallas kernels for 2%

profile of v4, /device:TPU:32, one launch (start us, length us, event | category | flops | bytes accessed | tf_op | source)
XLA Modules:
  0.0 114.7 jit_solution(12008346514769785181)
XLA Ops:
  0.0 4.4 %all-to-all-start = ((bf16[8,768,128]{2,1,0:T(8,128)(2,1)}), bf16[8,768,128]{2,1,0:T(8,128)(2,1)S(1)}, u32[]{:S(2)}, u32[]{:S(2)}) async-start(bf16[8,768,128]{2,1,0:T(8,128)(2,1)} %param.8), calls=%async_computation | async-start | bytes 3145728 | tf_op jit(solution)/shard_map/all_to_all | solution.py:118
  4.5 2.0 %collective-permute-start = (s32[1,8,8]{2,1,0:T(8,128)S(1)}, s32[1,8,8]{2,1,0:T(8,128)S(1)}, u32[]{:S(2)}, u32[]{:S(2)}) collective-permute-start(s32[1,8,8]{2,1,0:T(8,128)S(1)} %bitcast.13), channel_id=1, source_target_pairs={{0,32},{32,64},{64,96},{96,128},{128,160},{160,192},{192,224},{224... | collective-permute-start | bytes 776 | tf_op jit(solution)/shard_map/ppermute | solution.py:134
  6.5 1.7 %collective-permute-done = s32[1,8,8]{2,1,0:T(8,128)S(1)} collective-permute-done((s32[1,8,8]{2,1,0:T(8,128)S(1)}, s32[1,8,8]{2,1,0:T(8,128)S(1)}, u32[]{:S(2)}, u32[]{:S(2)}) %collective-permute-start) | collective-permute-done | bytes 288 | tf_op jit(solution)/shard_map/ppermute | solution.py:134
  8.1 4.1 %collective-permute-start.1 = (s32[2,8,8]{2,1,0:T(8,128)S(1)}, s32[2,8,8]{2,1,0:T(8,128)S(1)}, u32[]{:S(2)}, u32[]{:S(2)}) collective-permute-start(s32[2,8,8]{2,1,0:T(8,128)S(1)} %pad_add_fusion.2), channel_id=1, source_target_pairs={{0,64},{32,96},{64,128},{96,160},{128,192},{160,224},{192,0},{224,... | collective-permute-start | bytes 1544 | tf_op jit(solution)/shard_map/ppermute | solution.py:134
  12.3 2.9 %collective-permute-done.1 = s32[2,8,8]{2,1,0:T(8,128)S(1)} collective-permute-done((s32[2,8,8]{2,1,0:T(8,128)S(1)}, s32[2,8,8]{2,1,0:T(8,128)S(1)}, u32[]{:S(2)}, u32[]{:S(2)}) %collective-permute-start.1) | collective-permute-done | bytes 544 | tf_op jit(solution)/shard_map/ppermute | solution.py:134
  15.2 5.1 %collective-permute-start.2 = (s32[4,8,8]{2,1,0:T(8,128)S(1)}, s32[4,8,8]{2,1,0:T(8,128)S(1)}, u32[]{:S(2)}, u32[]{:S(2)}) collective-permute-start(s32[4,8,8]{2,1,0:T(8,128)S(1)} %pad_add_fusion.1), channel_id=1, source_target_pairs={{0,128},{32,160},{64,192},{96,224},{128,0},{160,32},{192,64},{224,... | collective-permute-start | bytes 3080 | tf_op jit(solution)/shard_map/ppermute | solution.py:134
  20.3 0.1 reshape.76.pattern_ref
  20.4 3.7 %copy-done.1 = bf16[8,768,768]{2,1,0:T(8,128)(2,1)S(1)} copy-done((bf16[8,768,768]{2,1,0:T(8,128)(2,1)S(1)}, bf16[8,768,768]{2,1,0:T(8,128)(2,1)}, u32[]{:S(2)}) %copy-start.1) | copy-done | bytes 9437208
  24.1 2.4 %mask.1.masked_ref = bf16[768,768]{1,0:T(8,128)(2,1)S(1)} custom-call(s32[1]{0:T(128)} %bitcast.4.tile_ref, s32[8,36]{1,0:T(8,128)S(1)} %reshape.76.pattern_ref, bf16[8,768,768]{2,1,0:T(8,128)(2,1)S(1)} %copy-done.1), custom_call_target="tpu_custom_call" | custom-call | tf_op jit(solution)/shard_map/mask/pallas_call | solution.py:120
  26.5 0.6 gather_fusion
  27.0 0.4 subtract_reduce_fusion
  27.5 0.1 copy.10
  27.6 0.1 reshape.78.target_ref
  27.6 0.2 copy.11.scale_ref
  27.8 2.7 %pair.1 = bf16[64,128,128]{2,1,0:T(8,128)(2,1)S(1)} custom-call(bf16[768,768]{1,0:T(8,128)(2,1)S(1)} %mask.1.masked_ref, bf16[8,768,128]{2,1,0:T(8,128)(2,1)S(1)} %all-to-all-done.border_ref, f32[768,1]{1,0:T(8,128)S(1)} %copy.11.scale_ref), custom_call_target="tpu_custom_call" | custom-call | tf_op jit(solution)/shard_map/pair/pallas_call | solution.py:143
  30.5 1.3 %copy-done.2 = bf16[64,128,128]{2,1,0:T(8,128)(2,1)} copy-done((bf16[64,128,128]{2,1,0:T(8,128)(2,1)}, bf16[64,128,128]{2,1,0:T(8,128)(2,1)S(1)}, u32[]{:S(2)}) %copy-start.2) | copy-done | bytes 2097176
  31.9 8.3 %all-to-all-start.1 = ((bf16[64,128,128]{2,1,0:T(8,128)(2,1)}), bf16[64,128,128]{2,1,0:T(8,128)(2,1)S(1)}, u32[]{:S(2)}, u32[]{:S(2)}) async-start(bf16[64,128,128]{2,1,0:T(8,128)(2,1)} %copy-done.2), calls=%async_computation.1 | async-start | bytes 4194304 | tf_op jit(solution)/shard_map/all_to_all | solution.py:152
  40.2 51.2 %all-to-all-done.1.in_ref = bf16[64,128,128]{2,1,0:T(8,128)(2,1)S(1)} async-done(((bf16[64,128,128]{2,1,0:T(8,128)(2,1)}), bf16[64,128,128]{2,1,0:T(8,128)(2,1)S(1)}, u32[]{:S(2)}, u32[]{:S(2)}) %all-to-all-start.1) | async-done | bytes 2097184 | tf_op jit(solution)/shard_map/all_to_all | solution.py:152
  91.4 1.4 %bins.1 = (bf16[16,128,128]{2,1,0:T(8,128)(2,1)S(1)}, bf16[8,128,128]{2,1,0:T(8,128)(2,1)S(1)}, bf16[8,128,128]{2,1,0:T(8,128)(2,1)S(1)}, bf16[8,128,128]{2,1,0:...) custom-call(s32[1]{0:T(128)} %bitcast.3.shift_ref, ...), custom_call_target="tpu_custom_call" | custom-call | tf_op jit(solution)/shard_map/bins/pallas_call | solution.py:154
  92.8 1.7 %collective-permute-start.3 = (bf16[8,128,128]{2,1,0:T(8,128)(2,1)S(1)}, bf16[8,128,128]{2,1,0:T(8,128)(2,1)S(1)}, u32[]{:S(2)}, u32[]{:S(2)}) collective-permute-start(bf16[8,128,128]{2,1,0:T(8,128)(2,1)S(1)} %get-tuple-element.22), channel_id=1, source_target_pairs={{0,8},{8,16},{16,24},{24,0},{1,9},{9,17},{17,25},{25,1},{2,10},{10... | collective-permute-start | bytes 786440 | tf_op jit(solution)/shard_map/ppermute | solution.py:166
  94.5 1.7 %collective-permute-start.7 = (bf16[8,128,128]{2,1,0:T(8,128)(2,1)S(1)}, bf16[8,128,128]{2,1,0:T(8,128)(2,1)S(1)}, u32[]{:S(2)}, u32[]{:S(2)}) collective-permute-start(bf16[8,128,128]{2,1,0:T(8,128)(2,1)S(1)} %get-tuple-element.26), channel_id=1, source_target_pairs={{0,24},{8,0},{16,8},{24,16},{1,25},{9,1},{17,9},{25,17},{2,26},{10... | collective-permute-start | bytes 786440 | tf_op jit(solution)/shard_map/ppermute | solution.py:166
  96.2 1.8 %collective-permute-start.5 = (bf16[8,128,128]{2,1,0:T(8,128)(2,1)S(1)}, bf16[8,128,128]{2,1,0:T(8,128)(2,1)S(1)}, u32[]{:S(2)}, u32[]{:S(2)}) collective-permute-start(bf16[8,128,128]{2,1,0:T(8,128)(2,1)S(1)} %get-tuple-element.23), channel_id=1, source_target_pairs={{0,24},{8,0},{16,8},{24,16},{1,25},{9,1},{17,9},{25,17},{2,26},{10... | collective-permute-start | bytes 786440 | tf_op jit(solution)/shard_map/ppermute | solution.py:166
  98.0 0.2 collective-permute-start.6
  98.2 5.0 %collective-permute-done.3 = bf16[8,128,128]{2,1,0:T(8,128)(2,1)S(1)} collective-permute-done((bf16[8,128,128]{2,1,0:T(8,128)(2,1)S(1)}, bf16[8,128,128]{2,1,0:T(8,128)(2,1)S(1)}, u32[]{:S(2)}, u32[]{:S(2)}) %collective-permute-start.3) | collective-permute-done | bytes 262176 | tf_op jit(solution)/shard_map/ppermute | solution.py:166
  103.1 0.1 add_convert_fusion.1
  103.2 0.7 collective-permute-start.4
  103.9 0.1 add_convert_fusion
  104.0 2.8 %collective-permute-start.8 = (bf16[8,128,128]{2,1,0:T(8,128)(2,1)S(1)}, bf16[8,128,128]{2,1,0:T(8,128)(2,1)S(1)}, u32[]{:S(2)}, u32[]{:S(2)}) collective-permute-start(bf16[8,128,128]{2,1,0:T(8,128)(2,1)S(1)} %add_convert_fusion), channel_id=1, source_target_pairs={{0,24},{8,0},{16,8},{24,16},{1,25},{9,1},{17,9},{25,17},{2,26},{10... | collective-permute-start | bytes 786440 | tf_op jit(solution)/shard_map/ppermute | solution.py:166
  106.8 0.1 pad_add_fusion.3.where_ref
  106.8 2.5 %collective-permute-done.5.down_a_ref = bf16[8,128,128]{2,1,0:T(8,128)(2,1)S(1)} collective-permute-done((bf16[8,128,128]{2,1,0:T(8,128)(2,1)S(1)}, bf16[8,128,128]{2,1,0:T(8,128)(2,1)S(1)}, u32[]{:S(2)}, u32[]{:S(2)}) %collective-permute-start.5) | collective-permute-done | bytes 262176 | tf_op jit(solution)/shard_map/ppermute | solution.py:166
  109.4 3.6 %collective-permute-done.4.up_a_ref = bf16[8,128,128]{2,1,0:T(8,128)(2,1)S(1)} collective-permute-done((bf16[8,128,128]{2,1,0:T(8,128)(2,1)S(1)}, bf16[8,128,128]{2,1,0:T(8,128)(2,1)S(1)}, u32[]{:S(2)}, u32[]{:S(2)}) %collective-permute-start.4) | collective-permute-done | bytes 262176 | tf_op jit(solution)/shard_map/ppermute | solution.py:166
  113.0 1.8 %final.1 = f32[1024,256]{1,0:T(8,128)} custom-call(s32[2]{0:T(128)S(1)} %pad_add_fusion.3.where_ref, f32[64,128]{1,0:T(8,128)S(1)} %bitcast.12, bf16[16,128,128]{2,1,0:T(8,128)(2,1)S(1)} %get-tuple-element.20.own_ref, bf16[8,128,128]{2,1,0:T(8,128)(2,1)S(1)} %collective-permute-done.4.up_a_ref, bf16[8,128,128]{2,1,0:T(8,128)(2,1)S(1)} %collective-permute-done.5.down_a_ref, ...), custom_call_target="tpu_custom_call" | custom-call | tf_op jit(solution)/shard_map/final/pallas_call | solution.py:175
  (23 shorter events, 0.1 us)
Async XLA Ops:
  0.0 20.3 %copy-start = (f32[8,768]{1,0:T(8,128)S(1)}, f32[8,768]{1,0:T(8,128)}, u32[]{:S(2)}) copy-start(f32[8,768]{1,0:T(8,128)} %param.9) | copy-start | bytes 73732
  0.0 4.5 %copy-start.4 = (s32[8,8]{1,0:T(8,128)S(1)}, s32[8,8]{1,0:T(8,128)}, u32[]{:S(2)}) copy-start(s32[8,8]{1,0:T(8,128)} %param.10) | copy-start | bytes 772
  0.0 20.3 %copy-start.5 = (s32[8,6,6]{2,0,1:T(8,128)S(1)}, s32[8,6,6]{2,0,1:T(8,128)}, u32[]{:S(2)}) copy-start(s32[8,6,6]{2,0,1:T(8,128)} %param.7) | copy-start | bytes 3460
  0.0 27.6 %all-to-all-start = ((bf16[8,768,128]{2,1,0:T(8,128)(2,1)}), bf16[8,768,128]{2,1,0:T(8,128)(2,1)S(1)}, u32[]{:S(2)}, u32[]{:S(2)}) async-start(bf16[8,768,128]{2,1,0:T(8,128)(2,1)} %param.8), calls=%async_computation | async-start | bytes 3145728 | tf_op jit(solution)/shard_map/all_to_all | solution.py:118
  4.5 3.7 %collective-permute-start = (s32[1,8,8]{2,1,0:T(8,128)S(1)}, s32[1,8,8]{2,1,0:T(8,128)S(1)}, u32[]{:S(2)}, u32[]{:S(2)}) collective-permute-start(s32[1,8,8]{2,1,0:T(8,128)S(1)} %bitcast.13), channel_id=1, source_target_pairs={{0,32},{32,64},{64,96},{96,128},{128,160},{160,192},{192,224},{224... | collective-permute-start | bytes 776 | tf_op jit(solution)/shard_map/ppermute | solution.py:134
  8.1 7.0 %collective-permute-start.1 = (s32[2,8,8]{2,1,0:T(8,128)S(1)}, s32[2,8,8]{2,1,0:T(8,128)S(1)}, u32[]{:S(2)}, u32[]{:S(2)}) collective-permute-start(s32[2,8,8]{2,1,0:T(8,128)S(1)} %pad_add_fusion.2), channel_id=1, source_target_pairs={{0,64},{32,96},{64,128},{96,160},{128,192},{160,224},{192,0},{224,... | collective-permute-start | bytes 1544 | tf_op jit(solution)/shard_map/ppermute | solution.py:134
  15.2 11.3 %collective-permute-start.2 = (s32[4,8,8]{2,1,0:T(8,128)S(1)}, s32[4,8,8]{2,1,0:T(8,128)S(1)}, u32[]{:S(2)}, u32[]{:S(2)}) collective-permute-start(s32[4,8,8]{2,1,0:T(8,128)S(1)} %pad_add_fusion.1), channel_id=1, source_target_pairs={{0,128},{32,160},{64,192},{96,224},{128,0},{160,32},{192,64},{224,... | collective-permute-start | bytes 3080 | tf_op jit(solution)/shard_map/ppermute | solution.py:134
  20.4 3.7 %copy-start.1 = (bf16[8,768,768]{2,1,0:T(8,128)(2,1)S(1)}, bf16[8,768,768]{2,1,0:T(8,128)(2,1)}, u32[]{:S(2)}) copy-start(bf16[8,768,768]{2,1,0:T(8,128)(2,1)} %factor_hbm.1) | copy-start | bytes 28311556
  30.5 1.3 %copy-start.2 = (bf16[64,128,128]{2,1,0:T(8,128)(2,1)}, bf16[64,128,128]{2,1,0:T(8,128)(2,1)S(1)}, u32[]{:S(2)}) copy-start(bf16[64,128,128]{2,1,0:T(8,128)(2,1)S(1)} %pair.1) | copy-start | bytes 6291460
  31.9 59.5 %all-to-all-start.1 = ((bf16[64,128,128]{2,1,0:T(8,128)(2,1)}), bf16[64,128,128]{2,1,0:T(8,128)(2,1)S(1)}, u32[]{:S(2)}, u32[]{:S(2)}) async-start(bf16[64,128,128]{2,1,0:T(8,128)(2,1)} %copy-done.2), calls=%async_computation.1 | async-start | bytes 4194304 | tf_op jit(solution)/shard_map/all_to_all | solution.py:152
  40.2 72.8 %copy-start.3 = (f32[8192]{0:T(1024)S(1)}, f32[8192]{0:T(1024)}, u32[]{:S(2)}) copy-start(f32[8192]{0:T(1024)} %param.11) | copy-start | bytes 98308
  92.8 10.3 %collective-permute-start.3 = (bf16[8,128,128]{2,1,0:T(8,128)(2,1)S(1)}, bf16[8,128,128]{2,1,0:T(8,128)(2,1)S(1)}, u32[]{:S(2)}, u32[]{:S(2)}) collective-permute-start(bf16[8,128,128]{2,1,0:T(8,128)(2,1)S(1)} %get-tuple-element.22), channel_id=1, source_target_pairs={{0,8},{8,16},{16,24},{24,0},{1,9},{9,17},{17,25},{25,1},{2,10},{10... | collective-permute-start | bytes 786440 | tf_op jit(solution)/shard_map/ppermute | solution.py:166
  94.5 9.4 %collective-permute-start.7 = (bf16[8,128,128]{2,1,0:T(8,128)(2,1)S(1)}, bf16[8,128,128]{2,1,0:T(8,128)(2,1)S(1)}, u32[]{:S(2)}, u32[]{:S(2)}) collective-permute-start(bf16[8,128,128]{2,1,0:T(8,128)(2,1)S(1)} %get-tuple-element.26), channel_id=1, source_target_pairs={{0,24},{8,0},{16,8},{24,16},{1,25},{9,1},{17,9},{25,17},{2,26},{10... | collective-permute-start | bytes 786440 | tf_op jit(solution)/shard_map/ppermute | solution.py:166
  96.2 13.2 %collective-permute-start.5 = (bf16[8,128,128]{2,1,0:T(8,128)(2,1)S(1)}, bf16[8,128,128]{2,1,0:T(8,128)(2,1)S(1)}, u32[]{:S(2)}, u32[]{:S(2)}) collective-permute-start(bf16[8,128,128]{2,1,0:T(8,128)(2,1)S(1)} %get-tuple-element.23), channel_id=1, source_target_pairs={{0,24},{8,0},{16,8},{24,16},{1,25},{9,1},{17,9},{25,17},{2,26},{10... | collective-permute-start | bytes 786440 | tf_op jit(solution)/shard_map/ppermute | solution.py:166
  98.0 11.4 %collective-permute-start.6 = (bf16[8,128,128]{2,1,0:T(8,128)(2,1)S(1)}, bf16[8,128,128]{2,1,0:T(8,128)(2,1)S(1)}, u32[]{:S(2)}, u32[]{:S(2)}) collective-permute-start(bf16[8,128,128]{2,1,0:T(8,128)(2,1)S(1)} %get-tuple-element.24), channel_id=1, source_target_pairs={{0,8},{8,16},{16,24},{24,0},{1,9},{9,17},{17,25},{25,1},{2,10},{10... | collective-permute-start | bytes 786440 | tf_op jit(solution)/shard_map/ppermute | solution.py:166
  103.2 9.7 %collective-permute-start.4 = (bf16[8,128,128]{2,1,0:T(8,128)(2,1)S(1)}, bf16[8,128,128]{2,1,0:T(8,128)(2,1)S(1)}, u32[]{:S(2)}, u32[]{:S(2)}) collective-permute-start(bf16[8,128,128]{2,1,0:T(8,128)(2,1)S(1)} %add_convert_fusion.1), channel_id=1, source_target_pairs={{0,8},{8,16},{16,24},{24,0},{1,9},{9,17},{17,25},{25,1},{2,10},{10... | collective-permute-start | bytes 786440 | tf_op jit(solution)/shard_map/ppermute | solution.py:166
  104.0 9.0 %collective-permute-start.8 = (bf16[8,128,128]{2,1,0:T(8,128)(2,1)S(1)}, bf16[8,128,128]{2,1,0:T(8,128)(2,1)S(1)}, u32[]{:S(2)}, u32[]{:S(2)}) collective-permute-start(bf16[8,128,128]{2,1,0:T(8,128)(2,1)S(1)} %add_convert_fusion), channel_id=1, source_target_pairs={{0,24},{8,0},{16,8},{24,16},{1,25},{9,1},{17,9},{25,17},{2,26},{10... | collective-permute-start | bytes 786440 | tf_op jit(solution)/shard_map/ppermute | solution.py:166

commit v5 on v4

--- a/solution.py
+++ b/solution.py
@@ -123,7 +123,7 @@
         in_specs=[SMEM, SMEM, HBM],
         out_specs=VMEM,
         scratch_shapes=[pltpu.VMEM((rows, rows), BF), pltpu.SemaphoreType.DMA((nblk,))],
-        compiler_params=PARAMS,
+        compiler_params=pltpu.CompilerParams(vmem_limit_bytes=48 << 20),
         name="mask",
     )(tile.reshape(1), pattern.reshape(local_scen, nblk * nblk), factor_inv)
     scale = lax.dynamic_slice_in_dim(row_scale, tile, 1, 0).reshape(rows, 1)

time: 117 us -> 117 us (level)
  local copies, waits for them, and re-layouts: 6.01 us -> 2.33 us
  waiting for transfers between devices: 66.8 us -> 69.3 us
  starting transfers between devices: 32.8 us -> 34.4 us
    unnamed x13 -> x11, local copies, waits for them, and re-layouts: 5.03 us -> 1.36 us
    all_to_all x1, waiting for transfers between devices: 0.01 us -> 2.05 us  [on_device(): borders = lax.all_to_all(border, ('x', 'core'), 0, 0, tiled=True)]
    all_to_all x1, starting transfers between devices: 8.31 us -> 9.92 us  [on_device(): received = lax.all_to_all(pairs, ('x', 'core', 'z'), 0, 0, tiled=True)]
  transfers between devices with their start and end apart: 11 -> 11, of which waited for: 6 -> 8; matrix products, arithmetic and copies ran while one was open for 1% -> 1% of each run, Pallas kernels for 2% -> 2%
where the time goes in v5:
time: 117 us; the launch traced here: 115 us
  waiting for transfers between devices  69.3 us (59%)
  starting transfers between devices  34.4 us (29%)
  Pallas kernels  7.93 us (7%)
  local copies, waits for them, and re-layouts  2.33 us (2%)
    all_to_all x1, waiting for transfers between devices, on_device(): received = lax.all_to_all(pairs, ('x', 'core', 'z'), 0, 0, tiled=True)  51.2 us
    ppermute x3, starting transfers between devices, on_device(): lax.ppermute(links, 'z', [(i, (i + step) % z_count) for i in range(z_coun...  11.2 us
    ppermute x6, waiting for transfers between devices, send(): lax.ppermute(value, 'y', [(k, (k + hop) % y_count) for k in range(y_count)])  11.1 us
    all_to_all x1, starting transfers between devices, on_device(): received = lax.all_to_all(pairs, ('x', 'core', 'z'), 0, 0, tiled=True)  9.92 us
    ppermute x6, starting transfers between devices, send(): lax.ppermute(value, 'y', [(k, (k + hop) % y_count) for k in range(y_count)])  8.82 us
    ppermute x3, waiting for transfers between devices, on_device(): lax.ppermute(links, 'z', [(i, (i + step) % z_count) for i in range(z_coun...  4.97 us
    all_to_all x1, starting transfers between devices, on_device(): borders = lax.all_to_all(border, ('x', 'core'), 0, 0, tiled=True)  4.44 us
    pallas_call x1, Pallas kernels, on_device(): pl.pallas_call(pair_kernel, out_shape=jax.ShapeDtypeStruct((groups * grou...  2.69 us
  transfers between devices with their start and end apart: 11, of which 8 were waited for; matrix products, arithmetic and copies ran while one was open for 1% of the time, Pallas kernels for 2%

profile of v5, /device:TPU:32, one launch (start us, length us, event | category | flops | bytes accessed | tf_op | source)
XLA Modules:
  0.0 114.8 jit_solution(4827768295000292701)
XLA Ops:
  0.0 4.4 %all-to-all-start = ((bf16[8,768,128]{2,1,0:T(8,128)(2,1)}), bf16[8,768,128]{2,1,0:T(8,128)(2,1)S(1)}, u32[]{:S(2)}, u32[]{:S(2)}) async-start(bf16[8,768,128]{2,1,0:T(8,128)(2,1)} %param.8), calls=%async_computation | async-start | bytes 3145728 | tf_op jit(solution)/shard_map/all_to_all | solution.py:118
  4.5 2.0 %collective-permute-start = (s32[1,8,8]{2,1,0:T(8,128)S(1)}, s32[1,8,8]{2,1,0:T(8,128)S(1)}, u32[]{:S(2)}, u32[]{:S(2)}) collective-permute-start(s32[1,8,8]{2,1,0:T(8,128)S(1)} %bitcast.13), channel_id=1, source_target_pairs={{0,32},{32,64},{64,96},{96,128},{128,160},{160,192},{192,224},{224... | collective-permute-start | bytes 776 | tf_op jit(solution)/shard_map/ppermute | solution.py:134
  6.5 1.7 %collective-permute-done = s32[1,8,8]{2,1,0:T(8,128)S(1)} collective-permute-done((s32[1,8,8]{2,1,0:T(8,128)S(1)}, s32[1,8,8]{2,1,0:T(8,128)S(1)}, u32[]{:S(2)}, u32[]{:S(2)}) %collective-permute-start) | collective-permute-done | bytes 288 | tf_op jit(solution)/shard_map/ppermute | solution.py:134
  8.1 4.1 %collective-permute-start.1 = (s32[2,8,8]{2,1,0:T(8,128)S(1)}, s32[2,8,8]{2,1,0:T(8,128)S(1)}, u32[]{:S(2)}, u32[]{:S(2)}) collective-permute-start(s32[2,8,8]{2,1,0:T(8,128)S(1)} %pad_add_fusion.2), channel_id=1, source_target_pairs={{0,64},{32,96},{64,128},{96,160},{128,192},{160,224},{192,0},{224,... | collective-permute-start | bytes 1544 | tf_op jit(solution)/shard_map/ppermute | solution.py:134
  12.3 2.9 %collective-permute-done.1 = s32[2,8,8]{2,1,0:T(8,128)S(1)} collective-permute-done((s32[2,8,8]{2,1,0:T(8,128)S(1)}, s32[2,8,8]{2,1,0:T(8,128)S(1)}, u32[]{:S(2)}, u32[]{:S(2)}) %collective-permute-start.1) | collective-permute-done | bytes 544 | tf_op jit(solution)/shard_map/ppermute | solution.py:134
  15.2 5.1 %collective-permute-start.2 = (s32[4,8,8]{2,1,0:T(8,128)S(1)}, s32[4,8,8]{2,1,0:T(8,128)S(1)}, u32[]{:S(2)}, u32[]{:S(2)}) collective-permute-start(s32[4,8,8]{2,1,0:T(8,128)S(1)} %pad_add_fusion.1), channel_id=1, source_target_pairs={{0,128},{32,160},{64,192},{96,224},{128,0},{160,32},{192,64},{224,... | collective-permute-start | bytes 3080 | tf_op jit(solution)/shard_map/ppermute | solution.py:134
  20.3 0.1 reshape.76.pattern_ref
  20.4 2.0 %mask.1.masked_ref = bf16[768,768]{1,0:T(8,128)(2,1)S(1)} custom-call(s32[1]{0:T(128)} %bitcast.4.tile_ref, s32[8,36]{1,0:T(8,128)S(1)} %reshape.76.pattern_ref, bf16[8,768,768]{2,1,0:T(8,128)(2,1)} %factor_hbm.1), custom_call_target="tpu_custom_call" | custom-call | tf_op jit(solution)/shard_map/mask/pallas_call | solution.py:120
  22.4 0.4 collective-permute-done.2
  22.8 0.6 gather_fusion
  23.4 0.4 subtract_reduce_fusion
  23.9 0.1 reshape.78.target_ref
  24.0 2.0 %all-to-all-done.border_ref = bf16[8,768,128]{2,1,0:T(8,128)(2,1)S(1)} async-done(((bf16[8,768,128]{2,1,0:T(8,128)(2,1)}), bf16[8,768,128]{2,1,0:T(8,128)(2,1)S(1)}, u32[]{:S(2)}, u32[]{:S(2)}) %all-to-all-start) | async-done | bytes 1572896 | tf_op jit(solution)/shard_map/all_to_all | solution.py:118
  26.0 0.2 copy.11.scale_ref
  26.2 2.7 %pair.1 = bf16[64,128,128]{2,1,0:T(8,128)(2,1)S(1)} custom-call(bf16[768,768]{1,0:T(8,128)(2,1)S(1)} %mask.1.masked_ref, bf16[8,768,128]{2,1,0:T(8,128)(2,1)S(1)} %all-to-all-done.border_ref, f32[768,1]{1,0:T(8,128)S(1)} %copy.11.scale_ref), custom_call_target="tpu_custom_call" | custom-call | tf_op jit(solution)/shard_map/pair/pallas_call | solution.py:143
  28.9 1.3 %copy-done.1 = bf16[64,128,128]{2,1,0:T(8,128)(2,1)} copy-done((bf16[64,128,128]{2,1,0:T(8,128)(2,1)}, bf16[64,128,128]{2,1,0:T(8,128)(2,1)S(1)}, u32[]{:S(2)}) %copy-start.1) | copy-done | bytes 2097176
  30.3 9.9 %all-to-all-start.1 = ((bf16[64,128,128]{2,1,0:T(8,128)(2,1)}), bf16[64,128,128]{2,1,0:T(8,128)(2,1)S(1)}, u32[]{:S(2)}, u32[]{:S(2)}) async-start(bf16[64,128,128]{2,1,0:T(8,128)(2,1)} %copy-done.1), calls=%async_computation.1 | async-start | bytes 4194304 | tf_op jit(solution)/shard_map/all_to_all | solution.py:152
  40.2 51.2 %all-to-all-done.1.in_ref = bf16[64,128,128]{2,1,0:T(8,128)(2,1)S(1)} async-done(((bf16[64,128,128]{2,1,0:T(8,128)(2,1)}), bf16[64,128,128]{2,1,0:T(8,128)(2,1)S(1)}, u32[]{:S(2)}, u32[]{:S(2)}) %all-to-all-start.1) | async-done | bytes 2097184 | tf_op jit(solution)/shard_map/all_to_all | solution.py:152
  91.4 1.4 %bins.1 = (bf16[16,128,128]{2,1,0:T(8,128)(2,1)S(1)}, bf16[8,128,128]{2,1,0:T(8,128)(2,1)S(1)}, bf16[8,128,128]{2,1,0:T(8,128)(2,1)S(1)}, bf16[8,128,128]{2,1,0:...) custom-call(s32[1]{0:T(128)} %bitcast.3.shift_ref, ...), custom_call_target="tpu_custom_call" | custom-call | tf_op jit(solution)/shard_map/bins/pallas_call | solution.py:154
  92.8 1.7 %collective-permute-start.3 = (bf16[8,128,128]{2,1,0:T(8,128)(2,1)S(1)}, bf16[8,128,128]{2,1,0:T(8,128)(2,1)S(1)}, u32[]{:S(2)}, u32[]{:S(2)}) collective-permute-start(bf16[8,128,128]{2,1,0:T(8,128)(2,1)S(1)} %get-tuple-element.22), channel_id=1, source_target_pairs={{0,8},{8,16},{16,24},{24,0},{1,9},{9,17},{17,25},{25,1},{2,10},{10... | collective-permute-start | bytes 786440 | tf_op jit(solution)/shard_map/ppermute | solution.py:166
  94.5 1.7 %collective-permute-start.7 = (bf16[8,128,128]{2,1,0:T(8,128)(2,1)S(1)}, bf16[8,128,128]{2,1,0:T(8,128)(2,1)S(1)}, u32[]{:S(2)}, u32[]{:S(2)}) collective-permute-start(bf16[8,128,128]{2,1,0:T(8,128)(2,1)S(1)} %get-tuple-element.26), channel_id=1, source_target_pairs={{0,24},{8,0},{16,8},{24,16},{1,25},{9,1},{17,9},{25,17},{2,26},{10... | collective-permute-start | bytes 786440 | tf_op jit(solution)/shard_map/ppermute | solution.py:166
  96.2 1.8 %collective-permute-start.5 = (bf16[8,128,128]{2,1,0:T(8,128)(2,1)S(1)}, bf16[8,128,128]{2,1,0:T(8,128)(2,1)S(1)}, u32[]{:S(2)}, u32[]{:S(2)}) collective-permute-start(bf16[8,128,128]{2,1,0:T(8,128)(2,1)S(1)} %get-tuple-element.23), channel_id=1, source_target_pairs={{0,24},{8,0},{16,8},{24,16},{1,25},{9,1},{17,9},{25,17},{2,26},{10... | collective-permute-start | bytes 786440 | tf_op jit(solution)/shard_map/ppermute | solution.py:166
  98.0 0.2 collective-permute-start.6
  98.2 4.9 %collective-permute-done.3 = bf16[8,128,128]{2,1,0:T(8,128)(2,1)S(1)} collective-permute-done((bf16[8,128,128]{2,1,0:T(8,128)(2,1)S(1)}, bf16[8,128,128]{2,1,0:T(8,128)(2,1)S(1)}, u32[]{:S(2)}, u32[]{:S(2)}) %collective-permute-start.3) | collective-permute-done | bytes 262176 | tf_op jit(solution)/shard_map/ppermute | solution.py:166
  103.1 0.1 add_convert_fusion.1
  103.2 0.7 collective-permute-start.4
  103.9 0.1 add_convert_fusion
  104.0 2.8 %collective-permute-start.8 = (bf16[8,128,128]{2,1,0:T(8,128)(2,1)S(1)}, bf16[8,128,128]{2,1,0:T(8,128)(2,1)S(1)}, u32[]{:S(2)}, u32[]{:S(2)}) collective-permute-start(bf16[8,128,128]{2,1,0:T(8,128)(2,1)S(1)} %add_convert_fusion), channel_id=1, source_target_pairs={{0,24},{8,0},{16,8},{24,16},{1,25},{9,1},{17,9},{25,17},{2,26},{10... | collective-permute-start | bytes 786440 | tf_op jit(solution)/shard_map/ppermute | solution.py:166
  106.8 0.1 pad_add_fusion.3.where_ref
  106.8 2.5 %collective-permute-done.5.down_a_ref = bf16[8,128,128]{2,1,0:T(8,128)(2,1)S(1)} collective-permute-done((bf16[8,128,128]{2,1,0:T(8,128)(2,1)S(1)}, bf16[8,128,128]{2,1,0:T(8,128)(2,1)S(1)}, u32[]{:S(2)}, u32[]{:S(2)}) %collective-permute-start.5) | collective-permute-done | bytes 262176 | tf_op jit(solution)/shard_map/ppermute | solution.py:166
  109.4 3.6 %collective-permute-done.4.up_a_ref = bf16[8,128,128]{2,1,0:T(8,128)(2,1)S(1)} collective-permute-done((bf16[8,128,128]{2,1,0:T(8,128)(2,1)S(1)}, bf16[8,128,128]{2,1,0:T(8,128)(2,1)S(1)}, u32[]{:S(2)}, u32[]{:S(2)}) %collective-permute-start.4) | collective-permute-done | bytes 262176 | tf_op jit(solution)/shard_map/ppermute | solution.py:166
  113.0 1.8 %final.1 = f32[1024,256]{1,0:T(8,128)} custom-call(s32[2]{0:T(128)S(1)} %pad_add_fusion.3.where_ref, f32[64,128]{1,0:T(8,128)S(1)} %bitcast.12, bf16[16,128,128]{2,1,0:T(8,128)(2,1)S(1)} %get-tuple-element.20.own_ref, bf16[8,128,128]{2,1,0:T(8,128)(2,1)S(1)} %collective-permute-done.4.up_a_ref, bf16[8,128,128]{2,1,0:T(8,128)(2,1)S(1)} %collective-permute-done.5.down_a_ref, ...), custom_call_target="tpu_custom_call" | custom-call | tf_op jit(solution)/shard_map/final/pallas_call | solution.py:175
  (21 shorter events, 0.2 us)
Async XLA Ops:
  0.0 20.3 %copy-start = (f32[8,768]{1,0:T(8,128)S(1)}, f32[8,768]{1,0:T(8,128)}, u32[]{:S(2)}) copy-start(f32[8,768]{1,0:T(8,128)} %param.9) | copy-start | bytes 73732
  0.0 4.5 %copy-start.3 = (s32[8,8]{1,0:T(8,128)S(1)}, s32[8,8]{1,0:T(8,128)}, u32[]{:S(2)}) copy-start(s32[8,8]{1,0:T(8,128)} %param.10) | copy-start | bytes 772
  0.0 20.3 %copy-start.4 = (s32[8,6,6]{2,0,1:T(8,128)S(1)}, s32[8,6,6]{2,0,1:T(8,128)}, u32[]{:S(2)}) copy-start(s32[8,6,6]{2,0,1:T(8,128)} %param.7) | copy-start | bytes 3460
  0.0 26.0 %all-to-all-start = ((bf16[8,768,128]{2,1,0:T(8,128)(2,1)}), bf16[8,768,128]{2,1,0:T(8,128)(2,1)S(1)}, u32[]{:S(2)}, u32[]{:S(2)}) async-start(bf16[8,768,128]{2,1,0:T(8,128)(2,1)} %param.8), calls=%async_computation | async-start | bytes 3145728 | tf_op jit(solution)/shard_map/all_to_all | solution.py:118
  4.5 3.7 %collective-permute-start = (s32[1,8,8]{2,1,0:T(8,128)S(1)}, s32[1,8,8]{2,1,0:T(8,128)S(1)}, u32[]{:S(2)}, u32[]{:S(2)}) collective-permute-start(s32[1,8,8]{2,1,0:T(8,128)S(1)} %bitcast.13), channel_id=1, source_target_pairs={{0,32},{32,64},{64,96},{96,128},{128,160},{160,192},{192,224},{224... | collective-permute-start | bytes 776 | tf_op jit(solution)/shard_map/ppermute | solution.py:134
  8.1 7.0 %collective-permute-start.1 = (s32[2,8,8]{2,1,0:T(8,128)S(1)}, s32[2,8,8]{2,1,0:T(8,128)S(1)}, u32[]{:S(2)}, u32[]{:S(2)}) collective-permute-start(s32[2,8,8]{2,1,0:T(8,128)S(1)} %pad_add_fusion.2), channel_id=1, source_target_pairs={{0,64},{32,96},{64,128},{96,160},{128,192},{160,224},{192,0},{224,... | collective-permute-start | bytes 1544 | tf_op jit(solution)/shard_map/ppermute | solution.py:134
  15.2 7.6 %collective-permute-start.2 = (s32[4,8,8]{2,1,0:T(8,128)S(1)}, s32[4,8,8]{2,1,0:T(8,128)S(1)}, u32[]{:S(2)}, u32[]{:S(2)}) collective-permute-start(s32[4,8,8]{2,1,0:T(8,128)S(1)} %pad_add_fusion.1), channel_id=1, source_target_pairs={{0,128},{32,160},{64,192},{96,224},{128,0},{160,32},{192,64},{224,... | collective-permute-start | bytes 3080 | tf_op jit(solution)/shard_map/ppermute | solution.py:134
  28.9 1.3 %copy-start.1 = (bf16[64,128,128]{2,1,0:T(8,128)(2,1)}, bf16[64,128,128]{2,1,0:T(8,128)(2,1)S(1)}, u32[]{:S(2)}) copy-start(bf16[64,128,128]{2,1,0:T(8,128)(2,1)S(1)} %pair.1) | copy-start | bytes 6291460
  30.3 61.1 %all-to-all-start.1 = ((bf16[64,128,128]{2,1,0:T(8,128)(2,1)}), bf16[64,128,128]{2,1,0:T(8,128)(2,1)S(1)}, u32[]{:S(2)}, u32[]{:S(2)}) async-start(bf16[64,128,128]{2,1,0:T(8,128)(2,1)} %copy-done.1), calls=%async_computation.1 | async-start | bytes 4194304 | tf_op jit(solution)/shard_map/all_to_all | solution.py:152
  40.2 72.8 %copy-start.2 = (f32[8192]{0:T(1024)S(1)}, f32[8192]{0:T(1024)}, u32[]{:S(2)}) copy-start(f32[8192]{0:T(1024)} %param.11) | copy-start | bytes 98308
  92.8 10.3 %collective-permute-start.3 = (bf16[8,128,128]{2,1,0:T(8,128)(2,1)S(1)}, bf16[8,128,128]{2,1,0:T(8,128)(2,1)S(1)}, u32[]{:S(2)}, u32[]{:S(2)}) collective-permute-start(bf16[8,128,128]{2,1,0:T(8,128)(2,1)S(1)} %get-tuple-element.22), channel_id=1, source_target_pairs={{0,8},{8,16},{16,24},{24,0},{1,9},{9,17},{17,25},{25,1},{2,10},{10... | collective-permute-start | bytes 786440 | tf_op jit(solution)/shard_map/ppermute | solution.py:166
  94.5 9.4 %collective-permute-start.7 = (bf16[8,128,128]{2,1,0:T(8,128)(2,1)S(1)}, bf16[8,128,128]{2,1,0:T(8,128)(2,1)S(1)}, u32[]{:S(2)}, u32[]{:S(2)}) collective-permute-start(bf16[8,128,128]{2,1,0:T(8,128)(2,1)S(1)} %get-tuple-element.26), channel_id=1, source_target_pairs={{0,24},{8,0},{16,8},{24,16},{1,25},{9,1},{17,9},{25,17},{2,26},{10... | collective-permute-start | bytes 786440 | tf_op jit(solution)/shard_map/ppermute | solution.py:166
  96.2 13.2 %collective-permute-start.5 = (bf16[8,128,128]{2,1,0:T(8,128)(2,1)S(1)}, bf16[8,128,128]{2,1,0:T(8,128)(2,1)S(1)}, u32[]{:S(2)}, u32[]{:S(2)}) collective-permute-start(bf16[8,128,128]{2,1,0:T(8,128)(2,1)S(1)} %get-tuple-element.23), channel_id=1, source_target_pairs={{0,24},{8,0},{16,8},{24,16},{1,25},{9,1},{17,9},{25,17},{2,26},{10... | collective-permute-start | bytes 786440 | tf_op jit(solution)/shard_map/ppermute | solution.py:166
  98.0 11.4 %collective-permute-start.6 = (bf16[8,128,128]{2,1,0:T(8,128)(2,1)S(1)}, bf16[8,128,128]{2,1,0:T(8,128)(2,1)S(1)}, u32[]{:S(2)}, u32[]{:S(2)}) collective-permute-start(bf16[8,128,128]{2,1,0:T(8,128)(2,1)S(1)} %get-tuple-element.24), channel_id=1, source_target_pairs={{0,8},{8,16},{16,24},{24,0},{1,9},{9,17},{17,25},{25,1},{2,10},{10... | collective-permute-start | bytes 786440 | tf_op jit(solution)/shard_map/ppermute | solution.py:166
  103.2 9.7 %collective-permute-start.4 = (bf16[8,128,128]{2,1,0:T(8,128)(2,1)S(1)}, bf16[8,128,128]{2,1,0:T(8,128)(2,1)S(1)}, u32[]{:S(2)}, u32[]{:S(2)}) collective-permute-start(bf16[8,128,128]{2,1,0:T(8,128)(2,1)S(1)} %add_convert_fusion.1), channel_id=1, source_target_pairs={{0,8},{8,16},{16,24},{24,0},{1,9},{9,17},{17,25},{25,1},{2,10},{10... | collective-permute-start | bytes 786440 | tf_op jit(solution)/shard_map/ppermute | solution.py:166
  104.0 9.0 %collective-permute-start.8 = (bf16[8,128,128]{2,1,0:T(8,128)(2,1)S(1)}, bf16[8,128,128]{2,1,0:T(8,128)(2,1)S(1)}, u32[]{:S(2)}, u32[]{:S(2)}) collective-permute-start(bf16[8,128,128]{2,1,0:T(8,128)(2,1)S(1)} %add_convert_fusion), channel_id=1, source_target_pairs={{0,24},{8,0},{16,8},{24,16},{1,25},{9,1},{17,9},{25,17},{2,26},{10... | collective-permute-start | bytes 786440 | tf_op jit(solution)/shard_map/ppermute | solution.py:166
